TPU v7x, 128 devices: a whole 4x4x4 slice. The times are simulated.
128 devices in a mesh: ctx: 16 (over y_lo, z, core), dp: 8 (over y_hi, x).
Axes of the slice: x: 4, y: 4 (y_hi: 2, y_lo: 2; y = y_hi * 2 + y_lo), z: 4, core: 2. Of those that a mesh axis runs over, the one named last changes fastest.
Arguments:
- hidden: bfloat16 [98304, 1024], P(('dp', 'ctx')), parts along dimension 0, may hold values from -4 to 4
- in_weight: bfloat16 [1024, 4384], replicated, may hold values from -0.1875 to 0.1875
- conv_weight: float32 [4, 2304], replicated, may hold values from -3 to 3
- conv_bias: float32 [2304], replicated, may hold values from -3 to 3
- step_bias: float32 [32], replicated, may hold values from -1 to 1
- decay_rate: float32 [32], replicated, may hold values from 8.138021e-06 to 0.05
- skip_gain: float32 [32], replicated, may hold values from 0.5 to 1.5
- norm_gain: float32 [2048], replicated, may hold values from 0.5 to 1.5
- out_weight: bfloat16 [2048, 1024], replicated, may hold values from -0.125 to 0.125
Outputs:
- mixed: bfloat16 [98304, 1024], P(('dp', 'ctx')), parts along dimension 0
There are 8 independent parts, one for each index of `dp`. A program takes and returns all parts, laid end to end along the dimension named above; an argument that names none is the same for every part. Nothing has to cross between parts.
All inputs are finite; a program needn't handle non-finite values.
Results may differ from a plain program's by a relative error of at most 0.0065.
Values may be sent and summed in bfloat16 or wider, within the bound.
A program may use at most 256 MiB of HBM per device.

v0:
```python
import jax
import jax.numpy as jnp
from jax import lax
from jax.sharding import PartitionSpec as P

GROUP = 256


def from_behind(block, axis, distance):
    devices = range(lax.axis_size(axis))
    route = [(i - distance, i) for i in devices if i - distance in devices]
    return lax.ppermute(block, axis, route)


def carried_in(value, axis, combine, identity):
    count, mine = (lax.axis_size(axis), lax.axis_index(axis))
    everything = jax.tree.map(lambda part: lax.all_gather(part, axis), value)
    start = jax.tree.map(
        lambda part, zero: jnp.broadcast_to(jnp.asarray(zero, part.dtype), part.shape),
        value,
        identity,
    )

    def step(k, before):
        reached = k < mine
        new = combine(before, jax.tree.map(lambda part: part[k], everything))
        return jax.tree.map(lambda a, b: jnp.where(reached, a, b), new, before)

    return lax.fori_loop(0, count, step, start)


def partner(block, axis, distance):
    count = lax.axis_size(axis)
    route = []
    for low in range(count):
        high = low | 1 << distance
        if high != low and high < count:
            route += [(low, high), (high, low)]
    return lax.ppermute(block, axis, route)


def carry_combine(earlier, later):
    return (earlier[0] + later[0], jnp.exp(later[0])[:, None, None] * earlier[1] + later[1])


def group_terms(pieces, step_bias, decay_rate, skip_gain, head_count, head_dim, state_width):
    xc_block, step_raw = pieces
    inner_width = head_count * head_dim
    length = xc_block.shape[0]
    values = xc_block[:, :inner_width].reshape(length, head_count, head_dim)
    b_matrix = xc_block[:, inner_width : inner_width + state_width]
    c_matrix = xc_block[:, inner_width + state_width :]
    step_size = jax.nn.softplus(step_raw.astype(jnp.float32) + step_bias[None, :])
    log_decay = jnp.cumsum(-step_size * decay_rate[None, :], axis=0)
    scores = jnp.dot(c_matrix, b_matrix.T, preferred_element_type=jnp.float32)
    positions = jnp.arange(length)
    causal = positions[:, None] >= positions[None, :]
    log_gap = jnp.where(causal[None], log_decay.T[:, :, None] - log_decay.T[:, None, :], -jnp.inf)
    mixing = (jnp.exp(log_gap) * scores[None] * step_size.T[:, None, :]).astype(jnp.bfloat16)
    within = jnp.einsum("hts,shp->thp", mixing, values, preferred_element_type=jnp.float32)
    within = within + skip_gain[None, :, None] * values.astype(jnp.float32)
    to_end = jnp.exp(log_decay[-1][None, :] - log_decay) * step_size
    weighted = (values.astype(jnp.float32) * to_end[:, :, None]).astype(jnp.bfloat16)
    summary = jnp.einsum("shp,sn->hpn", weighted, b_matrix, preferred_element_type=jnp.float32)
    return (within, log_decay, summary)


def strand(hidden, weights, edge_fn, carry_fn):
    in_weight, conv_weight, conv_bias, step_bias, decay_rate, skip_gain, norm_gain, out_weight = (
        weights
    )
    head_count = step_bias.shape[0]
    inner_width = out_weight.shape[0]
    head_dim = inner_width // head_count
    conv_width = conv_weight.shape[1]
    state_width = (conv_width - inner_width) // 2
    kernel = conv_weight.shape[0]
    length = hidden.shape[0]
    projected = jnp.dot(hidden, in_weight, preferred_element_type=jnp.float32).astype(jnp.bfloat16)
    gating = projected[:, :inner_width]
    conv_in = projected[:, inner_width : inner_width + conv_width]
    step_raw = projected[:, inner_width + conv_width :]
    edge_rows = edge_fn(conv_in[length - kernel + 1 :])
    padded = jnp.concatenate([edge_rows, conv_in], 0)
    filtered = jnp.zeros((length, conv_width), jnp.float32) + conv_bias[None, :]
    for tap_index in range(kernel):
        filtered = filtered + conv_weight[tap_index][None, :] * padded[
            tap_index : tap_index + length
        ].astype(jnp.float32)
    xc = jax.nn.silu(filtered).astype(jnp.bfloat16)
    group_count = length // GROUP
    xc_blocks = xc.reshape(group_count, GROUP, conv_width)

    def local_terms(pieces):
        return group_terms(
            pieces, step_bias, decay_rate, skip_gain, head_count, head_dim, state_width
        )

    within, log_decay, summary = lax.map(
        local_terms, (xc_blocks, step_raw.reshape(group_count, GROUP, head_count))
    )
    totals = log_decay[:, -1, :]

    def advance(running, element):
        total, update = element
        return (jnp.exp(total)[:, None, None] * running + update, running)

    start_state = jnp.zeros((head_count, head_dim, state_width), jnp.float32)
    local_end, entering = lax.scan(advance, start_state, (totals, summary))
    before = jnp.cumsum(totals, axis=0) - totals
    in_log, in_state = carry_fn((jnp.sum(totals, axis=0), local_end))
    entering = entering + jnp.exp(before)[:, :, None, None] * in_state[None]
    c_blocks = xc_blocks[:, :, inner_width + state_width :]
    carried = jnp.einsum(
        "ctn,chpn->cthp",
        c_blocks,
        entering.astype(jnp.bfloat16),
        preferred_element_type=jnp.float32,
    )
    carried = carried * jnp.exp(log_decay)[:, :, :, None]
    scanned = (within + carried).reshape(length, inner_width)
    gated_out = scanned * jax.nn.silu(gating.astype(jnp.float32))
    normed = (
        gated_out
        * lax.rsqrt(jnp.mean(gated_out * gated_out, axis=-1, keepdims=True) + 1e-05)
        * norm_gain[None, :]
    ).astype(jnp.bfloat16)
    return jnp.dot(normed, out_weight, preferred_element_type=jnp.float32).astype(jnp.bfloat16)


def local(
    hidden,
    in_weight,
    conv_weight,
    conv_bias,
    step_bias,
    decay_rate,
    skip_gain,
    norm_gain,
    out_weight,
):
    weights = (
        in_weight,
        conv_weight,
        conv_bias,
        step_bias,
        decay_rate,
        skip_gain,
        norm_gain,
        out_weight,
    )
    head_count = step_bias.shape[0]
    head_dim = out_weight.shape[0] // head_count
    state_width = (conv_weight.shape[1] - out_weight.shape[0]) // 2
    identity = (
        jnp.zeros((head_count,), jnp.float32),
        jnp.zeros((head_count, head_dim, state_width), jnp.float32),
    )
    forward = strand(
        hidden,
        weights,
        lambda edge: from_behind(edge, "ctx", 1),
        lambda summary_pair: carried_in(summary_pair, "ctx", carry_combine, identity),
    )
    mirrored = hidden
    for bit_index in range(lax.axis_size("ctx").bit_length() - 1):
        mirrored = partner(mirrored, "ctx", bit_index)
    reverse_hidden = jnp.flip(mirrored, 0)
    backward = strand(
        reverse_hidden,
        weights,
        lambda edge: from_behind(edge, "ctx", 1),
        lambda summary_pair: carried_in(summary_pair, "ctx", carry_combine, identity),
    )
    returned = jnp.flip(backward, 0)
    for bit_index in range(lax.axis_size("ctx").bit_length() - 1):
        returned = partner(returned, "ctx", bit_index)
    return (
        hidden.astype(jnp.float32) + forward.astype(jnp.float32) + returned.astype(jnp.float32)
    ).astype(jnp.bfloat16)


def solution(mesh):
    return jax.shard_map(
        local,
        mesh=mesh,
        in_specs=(P(("dp", "ctx"), None), P(), P(), P(), P(), P(), P(), P(), P()),
        out_specs=P(("dp", "ctx"), None),
        check_vma=False,
    )
```

profile of v0, /device:TPU:0, one launch (start us, length us, event | category | flops | bytes accessed | tf_op | source)
XLA Modules:
  0.0 555.9 jit_solution(9113917057339594454)
XLA Ops:
  6.5 3.6 collective-permute-done.1
  12.2 34.7 %collective-permute-done.2 = bf16[768,1024]{1,0:T(8,128)(2,1)S(1)} collective-permute-done((bf16[768,1024]{1,0:T(8,128)(2,1)S(1)}, bf16[768,1024]{1,0:T(8,128)(2,1)S(1)}, u32[]{:S(2)}, u32[]{:S(2)}) %collective-permute-start.2) | collective-permute-done | bytes 1572896 | tf_op jit(solution)/shard_map/ppermute | solution.py:39
  46.9 3.7 collective-permute-start.3
  50.6 33.9 %collective-permute-done.3 = bf16[768,1024]{1,0:T(8,128)(2,1)} collective-permute-done((bf16[768,1024]{1,0:T(8,128)(2,1)S(1)}, bf16[768,1024]{1,0:T(8,128)(2,1)}, u32[]{:S(2)}, u32[]{:S(2)}) %collective-permute-start.3) | collective-permute-done | bytes 1572896 | tf_op jit(solution)/shard_map/ppermute | solution.py:39
  86.1 10.3 %convolution_convert_fusion.1 = bf16[768,4384]{0,1:T(8,128)(2,1)S(1)} fusion(bf16[768,1024]{1,0:T(8,128)(2,1)} %param.21, bf16[1024,4384]{0,1:T(8,128)(2,1)} %param.22), kind=kOutput, calls=%fused_computation.103 | convolution fusion | flops 6898802688 | bytes 17285120 | tf_op jit(solution)/shard_map/dot_general | solution.py:79
  96.4 2.7 copy-done.2
  100.9 18.8 %collective-permute-done.4 = bf16[768,1024]{1,0:T(8,128)(2,1)S(1)} collective-permute-done((bf16[768,1024]{1,0:T(8,128)(2,1)}, bf16[768,1024]{1,0:T(8,128)(2,1)S(1)}, u32[]{:S(2)}, u32[]{:S(2)}) %collective-permute-start.4) | collective-permute-done | bytes 1572896 | tf_op jit(solution)/shard_map/ppermute | solution.py:39
  119.7 15.3 %rev.7 = bf16[768,1024]{1,0:T(8,128)(2,1)} reverse(bf16[768,1024]{1,0:T(8,128)(2,1)S(1)} %collective-permute-done.4), dimensions={0} | reverse | bytes 3145728 | tf_op jit(solution)/shard_map/jit(_flip)/rev | solution.py:168
  135.1 10.3 %convolution_convert_fusion = bf16[768,4384]{0,1:T(8,128)(2,1)S(1)} fusion(bf16[768,1024]{1,0:T(8,128)(2,1)} %rev.7, bf16[1024,4384]{0,1:T(8,128)(2,1)} %param.22), kind=kOutput, calls=%fused_computation.102 | convolution fusion | flops 6898802688 | bytes 17285120 | tf_op jit(solution)/shard_map/dot_general | solution.py:79
  145.4 2.7 copy-done.3
  150.2 4.0 slice.141
  154.5 4.0 slice.150
  158.9 25.1 %multiply_convert_fusion.9 = (bf16[768,2304]{0,1:T(8,128)(2,1)}, bf16[768,2304]{0,1:T(8,128)(2,1)}) fusion(bf16[768,2304]{0,1:T(8,128)(2,1)} %slice.141, bf16[3,2304]{0,1:T(8,128)(2,1)S(1)} %copy.63, f32[2304]{0:T(1024)S(1)} %get-tuple-element.509, f32[2304]{0:T(1024)S(1)} %get-tuple-element.510, f32[2304]{0:T(1024)S(1)} %get-tuple-element.508, ...), kind=kLoop, calls=%fused_computation.109 | loop fusion | flops 92012544 | bytes 14229504 | tf_op jit(solution)/shard_map/convert_element_type | solution.py:90
  184.0 5.8 %copy.69 = bf16[768,2304]{1,0:T(8,128)(2,1)} copy(bf16[768,2304]{0,1:T(8,128)(2,1)} %get-tuple-element.598) | data formatting | bytes 7077888 | tf_op jit(solution)/shard_map/convert_element_type | solution.py:90
  189.8 3.4 broadcast.86.clone
  193.2 2.1 broadcast.88.clone
  195.3 38.6 %while.83 = (s32[]{:T(128)}, f32[3,256,32,64]{1,3,2,0:T(8,128)}, f32[3,256,32]{1,2,0:T(8,128)S(1)}, f32[3,32,64,128]{3,2,1,0:T(8,128)}, bf16[3,256,2304]{2,1,0:T...) while((s32[]{:T(128)}, f32[3,256,32,64]{1,3,2,0:T(8,128)}, ...), condition=%wide.region_14.15_spmd, body=%wide.region_11.14_spmd.sunk | while | flops 434356320 | bytes 14229053 | solution.py:99
  202.1 4.5 fusion.134
  214.9 4.6 fusion.134
  227.9 4.5 fusion.134
  234.6 2.1 broadcast.88.clone.1
  236.7 7.5 %while.86 = (s32[]{:T(128)}, f32[32,64,128]{2,1,0:T(8,128)S(1)}, f32[3,32,64,128]{3,2,1,0:T(8,128)}, f32[3,32]{1,0:T(4,128)S(1)}, f32[3,32,64,128]{3,2,1,0:T(8,128)}, /*index=5*/s32[]{:T(128)}, s32[]{:T(128)}) while((s32[]{:T(128)}, f32[32,64,128]{2,1,0:T(8,128)S(1)}, f32[3,32,64,128]{3,2,1,0:T(8,128)}, f32[3,32]{1,0:T(4,128)S(1)}, ...), condition=%wide.region_16.17_spmd.clone, body=%wide.region_15.16_spmd.clone.sunk | while | flops 1048579 | bytes 5243872 | solution.py:109
  245.3 5.8 %copy.64 = bf16[768,2304]{1,0:T(8,128)(2,1)} copy(bf16[768,2304]{0,1:T(8,128)(2,1)} %get-tuple-element.597) | data formatting | bytes 7077888 | tf_op jit(solution)/shard_map/convert_element_type | solution.py:90
  251.1 3.4 broadcast.86.clone.1
  257.2 38.4 %while.82 = (s32[]{:T(128)}, f32[3,256,32,64]{1,3,2,0:T(8,128)}, f32[3,256,32]{1,2,0:T(8,128)}, f32[3,32,64,128]{3,2,1,0:T(8,128)}, bf16[3,256,2304]{2,1,0:T(8,1...) while((s32[]{:T(128)}, f32[3,256,32,64]{1,3,2,0:T(8,128)}, ...), condition=%wide.region_3.4_spmd, body=%wide.region_0.3_spmd.sunk | while | flops 434356320 | bytes 14226689 | solution.py:99
  264.0 3.9 fusion.125
  276.8 3.9 fusion.125
  289.6 3.9 fusion.125
  296.7 2.1 broadcast.88.clone.3
  298.8 7.7 %while.84 = (s32[]{:T(128)}, f32[32,64,128]{2,1,0:T(8,128)S(1)}, f32[3,32,64,128]{3,2,1,0:T(8,128)}, f32[3,32]{1,0:T(4,128)S(1)}, f32[3,32,64,128]{3,2,1,0:T(8,128)}, /*index=5*/s32[]{:T(128)}, s32[]{:T(128)}) while((s32[]{:T(128)}, f32[32,64,128]{2,1,0:T(8,128)S(1)}, f32[3,32,64,128]{3,2,1,0:T(8,128)}, f32[3,32]{1,0:T(4,128)S(1)}, ...), condition=%wide.region_5.6_spmd.clone, body=%wide.region_4.5_spmd.clone.sunk | while | flops 1048579 | bytes 5243872 | solution.py:109
  309.3 31.1 %all-reduce.2 = (f32[512]{0:T(512)S(1)}, f32[512]{0:T(512)S(1)}) all-reduce(f32[512]{0:T(512)S(1)} %dynamic-update-slice.1, f32[512]{0:T(512)S(1)} %dynamic-update-slice), channel_id=4, replica_groups=mesh['ctx'=16,'dp'=8] {'ctx'}, use_global_device_ids=true, to_apply=%add.1 | all-reduce | flops 1024 | bytes 8192
  340.6 24.3 %while.87 = (s32[]{:T(128)}, f32[32,64,128]{2,1,0:T(8,128)S(1)}, s32[]{:T(128)}, f32[16,32]{1,0:T(8,128)S(1)}, f32[16,32,64,128]{3,2,1,0:T(8,128)}, /*index=5*/s32[]{:T(128)}, s32[]{:T(128)}) while((s32[]{:T(128)}, f32[32,64,128]{2,1,0:T(8,128)S(1)}, s32[]{:T(128)}, f32[16,32]{1,0:T(8,128)S(1)}, f32[16,32,64,128]{3,2,1,0:T(8,128)}, ...), condition=%wide.region_20.21_spmd.clone, body=%wide.region_19.20_spmd.clone.sunk | while | flops 1048580 | bytes 3146217 | solution.py:29
  364.9 7.7 %multiply_add_fusion = f32[3,256,32,64]{1,3,2,0:T(8,128)} fusion(f32[3,256,32,64]{1,3,2,0:T(8,128)} %get-tuple-element.353, f32[3,256,32]{1,2,0:T(8,128)S(1)} %exp.107, f32[3,32,64,128]{3,2,1,0:T(8,128)} %get-tuple-element.356, f32[32,64,128]{2,1,0:T(8,128)S(1)} %get-tuple-element.358, f32[3,32]{1,0:T(4,128)S(1)} %subtract_exponential_fusion, ...), kind=kOutput, calls=%fused_computation.120 | convolution fusion | flops 408158208 | bytes 17072512 | tf_op jit(solution)/shard_map/ctn,chpn->cthp/dot_general | solution.py:114
  372.6 8.0 %copy.71 = f32[3,256,32,64]{1,0,3,2:T(4,128)S(1)} copy(f32[3,256,32,64]{1,3,2,0:T(8,128)} %multiply_add_fusion) | data formatting | bytes 12582912 | tf_op jit(solution)/shard_map/add | solution.py:121
  382.2 4.1 multiply_reduce_fusion
  386.3 7.5 %fusion.80 = bf16[768,1024]{1,0:T(8,128)(2,1)} fusion(bf16[2048,1024]{1,0:T(8,128)(2,1)S(1)} %copy-done.14, f32[768]{0:T(1024)S(1)} %add_rsqrt_fusion, f32[2048]{0:T(1024)S(1)} %copy-done.16, f32[768,2048]{0,1:T(8,128)S(1)} %bitcast.282, bf16[768,4384]{0,1:T(8,128)(2,1)} %copy-done.3), kind=kOutput, calls=%fused_computation.147 | convolution fusion | flops 3236167680 | bytes 15215616 | tf_op jit(solution)/shard_map/dot_general | solution.py:128
  393.8 19.0 %rev.8 = bf16[768,1024]{1,0:T(8,128)(2,1)S(1)} reverse(bf16[768,1024]{1,0:T(8,128)(2,1)} %fusion.80), dimensions={0} | reverse | bytes 3145728 | tf_op jit(solution)/shard_map/jit(_flip)/rev | solution.py:175
  414.2 2.6 collective-permute-done.6
  418.3 29.8 %all-gather.7.cloned.1.call-done = f32[512,64,128]{2,1,0:T(8,128)} async-done(((f32[32,64,128]{2,1,0:T(8,128)}), f32[512,64,128]{2,1,0:T(8,128)}) %all-gather.7.cloned.1.call-update) | async-done | bytes 16777232 | tf_op jit(solution)/shard_map/all_gather | solution.py:17
  448.1 24.0 %while.85 = (s32[]{:T(128)}, f32[32,64,128]{2,1,0:T(8,128)S(1)}, s32[]{:T(128)}, f32[16,32]{1,0:T(8,128)S(1)}, f32[16,32,64,128]{3,2,1,0:T(8,128)}, /*index=5*/s32[]{:T(128)}, s32[]{:T(128)}) while((s32[]{:T(128)}, f32[32,64,128]{2,1,0:T(8,128)S(1)}, s32[]{:T(128)}, f32[16,32]{1,0:T(8,128)S(1)}, f32[16,32,64,128]{3,2,1,0:T(8,128)}, ...), condition=%wide.region_9.10_spmd.clone, body=%wide.region_8.9_spmd.clone.sunk | while | flops 1048580 | bytes 3146217 | solution.py:29
  472.1 2.9 collective-permute-start.8
  475.1 7.4 %multiply_add_fusion.1 = f32[3,256,32,64]{1,3,2,0:T(8,128)} fusion(f32[3,256,32,64]{1,3,2,0:T(8,128)} %get-tuple-element.347, f32[3,256,32]{1,2,0:T(8,128)S(1)} %exp.103, f32[3,32,64,128]{3,2,1,0:T(8,128)} %get-tuple-element.350, f32[32,64,128]{2,1,0:T(8,128)S(1)} %get-tuple-element.352, f32[3,32]{1,0:T(4,128)S(1)} %subtract_exponential_fusion.1, ...), kind=kOutput, calls=%fused_computation.123 | convolution fusion | flops 408158208 | bytes 17072512 | tf_op jit(solution)/shard_map/ctn,chpn->cthp/dot_general | solution.py:114
  482.5 7.9 %copy.66 = f32[3,256,32,64]{1,0,3,2:T(4,128)S(1)} copy(f32[3,256,32,64]{1,3,2,0:T(8,128)} %multiply_add_fusion.1) | data formatting | bytes 12582912 | tf_op jit(solution)/shard_map/add | solution.py:121
  492.0 3.7 multiply_reduce_fusion.1
  495.7 14.9 %collective-permute-done.8 = bf16[768,1024]{1,0:T(8,128)(2,1)} collective-permute-done((bf16[768,1024]{1,0:T(8,128)(2,1)}, bf16[768,1024]{1,0:T(8,128)(2,1)}, u32[]{:S(2)}, u32[]{:S(2)}) %collective-permute-start.8) | collective-permute-done | bytes 1572896 | tf_op jit(solution)/shard_map/ppermute | solution.py:39
  511.7 6.2 %fusion.81 = bf16[768,1024]{1,0:T(8,128)(2,1)S(1)} fusion(bf16[2048,1024]{1,0:T(8,128)(2,1)S(1)} %copy-done.15, f32[2048]{0:T(1024)S(1)} %copy-done.16, f32[768]{0:T(1024)S(1)} %add_rsqrt_fusion.1, f32[768,2048]{0,1:T(8,128)S(1)} %bitcast.280, bf16[768,4384]{0,1:T(8,128)(2,1)} %copy-done.2), kind=kOutput, calls=%fused_computation.148 | convolution fusion | flops 3236167680 | bytes 15215616 | tf_op jit(solution)/shard_map/dot_general | solution.py:128
  517.8 28.8 %collective-permute-done.9 = bf16[768,1024]{1,0:T(8,128)(2,1)S(1)} collective-permute-done((bf16[768,1024]{1,0:T(8,128)(2,1)}, bf16[768,1024]{1,0:T(8,128)(2,1)S(1)}, u32[]{:S(2)}, u32[]{:S(2)}) %collective-permute-start.9) | collective-permute-done | bytes 1572896 | tf_op jit(solution)/shard_map/ppermute | solution.py:39
  546.7 2.2 add_convert_fusion
  (271 shorter events, 136.9 us)
Async XLA Ops:
  6.5 334.1 %all-gather.9.cloned.1.call-start = ((), (), s32[]{:S(2)}) async-start(), calls=%async_computation.1 | async-start | bytes 17825792 | tf_op jit(solution)/shard_map/all_gather | solution.py:17
  6.5 3.6 collective-permute-start.1
  10.2 36.7 %collective-permute-start.2 = (bf16[768,1024]{1,0:T(8,128)(2,1)S(1)}, bf16[768,1024]{1,0:T(8,128)(2,1)S(1)}, u32[]{:S(2)}, u32[]{:S(2)}) collective-permute-start(bf16[768,1024]{1,0:T(8,128)(2,1)S(1)} %collective-permute-done.1), channel_id=1, source_target_pairs={{0,16},{16,0},{8,24},{24,8},{32,48},{48,32},{40,56},{56,40},{64,80... | collective-permute-start | bytes 4718600 | tf_op jit(solution)/shard_map/ppermute | solution.py:39
  46.9 37.6 %collective-permute-start.3 = (bf16[768,1024]{1,0:T(8,128)(2,1)S(1)}, bf16[768,1024]{1,0:T(8,128)(2,1)}, u32[]{:S(2)}, u32[]{:S(2)}) collective-permute-start(bf16[768,1024]{1,0:T(8,128)(2,1)S(1)} %collective-permute-done.2), channel_id=1, source_target_pairs={{0,32},{32,0},{8,40},{40,8},{16,48},{48,16},{24,56},{56,24},{64,96... | collective-permute-start | bytes 4718600 | tf_op jit(solution)/shard_map/ppermute | solution.py:39
  84.5 35.2 %collective-permute-start.4 = (bf16[768,1024]{1,0:T(8,128)(2,1)}, bf16[768,1024]{1,0:T(8,128)(2,1)S(1)}, u32[]{:S(2)}, u32[]{:S(2)}) collective-permute-start(bf16[768,1024]{1,0:T(8,128)(2,1)} %collective-permute-done.3), channel_id=1, source_target_pairs={{0,64},{64,0},{8,72},{72,8},{16,80},{80,16},{24,88},{88,24},{32,96... | collective-permute-start | bytes 4718600 | tf_op jit(solution)/shard_map/ppermute | solution.py:39
  96.4 2.8 copy-start.2
  99.6 54.6 %collective-permute-start = (bf16[3,2304]{1,0:T(4,128)(2,1)S(1)}, bf16[3,2304]{1,0:T(4,128)(2,1)S(1)}, u32[]{:S(2)}, u32[]{:S(2)}) collective-permute-start(bf16[3,2304]{1,0:T(4,128)(2,1)S(1)} %copy.62), channel_id=1, source_target_pairs={{0,8},{8,16},{16,24},{24,32},{32,40},{40,48},{48,56},{56,64},{64,7... | collective-permute-start | bytes 41480 | tf_op jit(solution)/shard_map/ppermute | solution.py:12
  135.1 15.0 %copy-start.9 = (f32[4,2304]{1,0:T(4,128)S(1)}, f32[4,2304]{1,0:T(4,128)}, u32[]{:S(2)}) copy-start(f32[4,2304]{1,0:T(4,128)} %param.23) | copy-start | bytes 110596
  145.3 2.8 copy-start.3
  148.6 10.0 %collective-permute-start.5 = (bf16[3,2304]{1,0:T(4,128)(2,1)S(1)}, bf16[3,2304]{1,0:T(4,128)(2,1)S(1)}, u32[]{:S(2)}, u32[]{:S(2)}) collective-permute-start(bf16[3,2304]{1,0:T(4,128)(2,1)S(1)} %copy.67), channel_id=1, source_target_pairs={{0,8},{8,16},{16,24},{24,32},{32,40},{40,48},{48,56},{56,64},{64,7... | collective-permute-start | bytes 41480 | tf_op jit(solution)/shard_map/ppermute | solution.py:12
  150.2 8.4 %slice-start.1 = ((bf16[768,4384]{0,1:T(8,128)(2,1)}), bf16[768,32]{0,1:T(8,128)(2,1)S(1)}, s32[]{:S(2)}) async-start(bf16[768,4384]{0,1:T(8,128)(2,1)} %copy-done.3), calls=%async_computation.3 | async-start | bytes 98304 | tf_op jit(solution)/shard_map/slice | solution.py:82
  150.2 8.8 %copy-start.12 = (f32[2304]{0:T(1024)S(1)}, f32[2304]{0:T(1024)}, u32[]{:S(2)}) copy-start(f32[2304]{0:T(1024)} %param.24) | copy-start | bytes 27652
  196.9 1.0 copy-start.7
  202.1 6.0 %copy-start.8 = (f32[32,2]{0,1:T(2,128)S(1)}, f32[32,2]{0,1:T(2,128)}, u32[]{:S(2)}) copy-start(f32[32,2]{0,1:T(2,128)} %copy-done.7) | copy-start | bytes 772 | tf_op jit(solution)/shard_map/while
  209.7 1.0 copy-start.7
  214.9 6.1 %copy-start.8 = (f32[32,2]{0,1:T(2,128)S(1)}, f32[32,2]{0,1:T(2,128)}, u32[]{:S(2)}) copy-start(f32[32,2]{0,1:T(2,128)} %copy-done.7) | copy-start | bytes 772 | tf_op jit(solution)/shard_map/while
  222.6 1.0 copy-start.7
  227.8 6.0 %copy-start.8 = (f32[32,2]{0,1:T(2,128)S(1)}, f32[32,2]{0,1:T(2,128)}, u32[]{:S(2)}) copy-start(f32[32,2]{0,1:T(2,128)} %copy-done.7) | copy-start | bytes 772 | tf_op jit(solution)/shard_map/while
  233.9 2.8 copy-start.5
  236.7 8.6 %slice-start = ((bf16[768,4384]{0,1:T(8,128)(2,1)}), bf16[768,32]{0,1:T(8,128)(2,1)S(1)}, s32[]{:S(2)}) async-start(bf16[768,4384]{0,1:T(8,128)(2,1)} %copy-done.2), calls=%async_computation.2 | async-start | bytes 98304 | tf_op jit(solution)/shard_map/slice | solution.py:82
  244.2 1.0 copy-start
  244.2 1.0 copy-start.10
  245.2 202.9 %all-gather.7.cloned.1.call-start = ((), (), s32[]{:S(2)}) async-start(), calls=%async_computation | async-start | bytes 17825792 | tf_op jit(solution)/shard_map/all_gather | solution.py:17
  251.1 6.1 %copy-start.17 = (f32[32]{0:T(128)S(1)}, f32[32]{0:T(128)}, u32[]{:S(2)}) copy-start(f32[32]{0:T(128)} %get-tuple-element.1023) | copy-start | bytes 388
  298.8 8.7 %copy-start.18 = (u32[128]{0:T(128)S(1)}, u32[128]{0:T(128)}, u32[]{:S(2)}) copy-start(u32[128]{0:T(128)} %constant.133) | copy-start | bytes 1540
  298.8 10.0 %copy-start.6 = (f32[3,256,32]{1,2,0:T(8,128)S(1)}, f32[3,256,32]{1,2,0:T(8,128)}, u32[]{:S(2)}) copy-start(f32[3,256,32]{1,2,0:T(8,128)} %copy-done.5) | copy-start | bytes 294916
  298.8 10.3 %copy-start.13 = (f32[32]{0:T(128)S(1)}, f32[32]{0:T(128)}, u32[]{:S(2)}) copy-start(f32[32]{0:T(128)} %get-tuple-element.505) | copy-start | bytes 388
  298.8 41.7 %copy-start.11 = (f32[3,32]{1,0:T(4,128)S(1)}, f32[3,32]{1,0:T(4,128)}, u32[]{:S(2)}) copy-start(f32[3,32]{1,0:T(4,128)} %copy-done.10) | copy-start | bytes 1156
  306.5 1.0 copy-start.1
  382.1 4.1 copy-start.14
  382.1 4.1 copy-start.16
  412.8 4.0 collective-permute-start.6
  416.8 55.4 %collective-permute-start.7 = (bf16[768,1024]{1,0:T(8,128)(2,1)}, bf16[768,1024]{1,0:T(8,128)(2,1)}, u32[]{:S(2)}, u32[]{:S(2)}) collective-permute-start(bf16[768,1024]{1,0:T(8,128)(2,1)} %collective-permute-done.6), channel_id=1, source_target_pairs={{0,16},{16,0},{8,24},{24,8},{32,48},{48,32},{40,56},{56,40},{64,80... | collective-permute-start | bytes 4718600 | tf_op jit(solution)/shard_map/ppermute | solution.py:39
  472.1 38.5 %collective-permute-start.8 = (bf16[768,1024]{1,0:T(8,128)(2,1)}, bf16[768,1024]{1,0:T(8,128)(2,1)}, u32[]{:S(2)}, u32[]{:S(2)}) collective-permute-start(bf16[768,1024]{1,0:T(8,128)(2,1)} %collective-permute-done.7), channel_id=1, source_target_pairs={{0,32},{32,0},{8,40},{40,8},{16,48},{48,16},{24,56},{56,24},{64,96... | collective-permute-start | bytes 4718600 | tf_op jit(solution)/shard_map/ppermute | solution.py:39
  492.0 19.7 %copy-start.15 = (bf16[2048,1024]{1,0:T(8,128)(2,1)S(1)}, bf16[2048,1024]{1,0:T(8,128)(2,1)}, u32[]{:S(2)}) copy-start(bf16[2048,1024]{1,0:T(8,128)(2,1)} %param.29) | copy-start | bytes 12582916
  495.7 50.9 %copy-start.4 = (bf16[768,1024]{1,0:T(8,128)(2,1)S(1)}, bf16[768,1024]{1,0:T(8,128)(2,1)}, u32[]{:S(2)}) copy-start(bf16[768,1024]{1,0:T(8,128)(2,1)} %param.21) | copy-start | bytes 4718596
  510.6 36.1 %collective-permute-start.9 = (bf16[768,1024]{1,0:T(8,128)(2,1)}, bf16[768,1024]{1,0:T(8,128)(2,1)S(1)}, u32[]{:S(2)}, u32[]{:S(2)}) collective-permute-start(bf16[768,1024]{1,0:T(8,128)(2,1)} %collective-permute-done.8), channel_id=1, source_target_pairs={{0,64},{64,0},{8,72},{72,8},{16,80},{80,16},{24,88},{88,24},{32,96... | collective-permute-start | bytes 4718600 | tf_op jit(solution)/shard_map/ppermute | solution.py:39
Sparse Core Ops, SparseCore 0:
  245.3 95.2 all-gather.8
  342.3 105.7 all-gather.6
where the time goes:
time: 567 us; the launch traced here: 556 us
  waiting for transfers between devices  167 us (29%)
  local copies, waits for them, and re-layouts  126 us (22%)
  other arithmetic  115 us (20%)
  matrix products  84.3 us (15%)
  blocking collectives  31.1 us (5%)
  starting transfers between devices  16 us (3%)
  between operations  14.6 us (3%)
    ppermute x8, waiting for transfers between devices, partner(): return lax.ppermute(block, axis, route)  137 us
    select_n x32, other arithmetic, step(): return jax.tree.map(lambda a, b: jnp.where(reached, a, b), new, before)  47 us
    unnamed x1, blocking collectives  31.1 us
    all_gather x2, waiting for transfers between devices, carried_in(): everything = jax.tree.map(lambda part: lax.all_gather(part, axis), value)  29.8 us
    dot_general x6, matrix products, group_terms(): jnp.einsum('hts,shp->thp', mixing, values, preferred_element_type=jnp.flo...  25.2 us
    convert_element_type x1, other arithmetic, strand(): xc = jax.nn.silu(filtered).astype(jnp.bfloat16)  25.1 us
    dot_general x2, matrix products, strand(): jnp.dot(hidden, in_weight, preferred_element_type=jnp.float32)  20.5 us
    rev x1, local copies, waits for them, and re-layouts, local(): returned = jnp.flip(backward, 0)  19 us
  transfers between devices with their start and end apart: 12, of which 8 were waited for; matrix products, arithmetic and copies ran while one was open for 41% of the time, Pallas kernels for 0%

commit v1 on v0

v1 whole, which is shorter than its diff:
```python
import functools

import jax
import jax.numpy as jnp
from jax import lax
from jax.experimental import pallas as pl
from jax.experimental.pallas import tpu as pltpu
from jax.sharding import PartitionSpec as P

CHUNK = 128
TILE = 256
HALO = 8
ROWS = 256
LIMIT = 40.0
MESH = pl.DeviceIdType.MESH
HIGHEST = lax.Precision.HIGHEST
F32 = jnp.float32
BF16 = jnp.bfloat16


def dot(a, b):
    return jnp.dot(a, b, preferred_element_type=F32)


def dot_nt(a, b):
    return lax.dot_general(a, b, (((1,), (1,)), ((), ())), preferred_element_type=F32)


def silu(x):
    half = 0.5 * x
    return half + half * jnp.tanh(half)


def iota(shape, dim):
    return lax.broadcasted_iota(jnp.int32, shape, dim)


def high_low(x, heads):
    high = x.astype(BF16).astype(F32)
    return (high + pltpu.roll(x - high, heads, 1)).astype(BF16)


def spread_matrix(first_head, heads, head_dim, terms):
    row, column = iota((128, TILE), 0), iota((128, TILE), 1)
    head = first_head + lax.div(column, head_dim)
    hit = row == head
    if terms == 2:
        hit = hit | (row == head + heads)
    return jnp.where(hit, 1.0, 0.0)


def triangle(lower):
    row, column = iota((CHUNK, CHUNK), 0), iota((CHUNK, CHUNK), 1)
    return row >= column if lower else row <= column


def front_kernel(
    heads, head_dim, state, inner, x_ref, next_ref, prev_ref, w_ref, wdt_ref, cw_ref, cb_ref, bias_ref, decay_ref, skip_ref,
    gate_ref, xf_ref, xb_ref, yf_ref, yb_ref, sf_ref, sb_ref, end_ref, ef_ref, eb_ref, step_ref, tot_ref, span_ref,
    hx, xs, par, wf, wb, of, ob, gcf, gcb, btf, btb, small,
):
    length = x_ref.shape[0]
    chunks = length // CHUNK
    tiles = inner // TILE
    j = pl.program_id(0)

    def project():
        out = dot(hx[...], w_ref[...])
        xs[HALO : HALO + length] = out[:length]
        xs[HALO + length :] = out[length : length + HALO]
        xs[:HALO] = out[length + HALO :]

    def convolved(c):
        at = HALO + c * CHUNK
        taps = [cw_ref[k : k + 1, :] for k in range(4)]
        base = xs[at : at + CHUNK] * taps[3] + cb_ref[...]
        forward, backward = base, base
        for k in range(1, 4):
            forward = forward + xs[at - k : at - k + CHUNK] * taps[3 - k]
            backward = backward + xs[at + k : at + k + CHUNK] * taps[3 - k]
        return silu(forward), silu(backward)

    @pl.when(j == 0)
    def _():
        hx[:length] = x_ref[...]
        hx[length:] = jnp.concatenate(
            [next_ref[...].astype(F32), prev_ref[...].astype(F32)], 0
        ).astype(BF16)
        par[...] = jnp.zeros_like(par)
        par[0:1, :heads] = bias_ref[...]
        par[1:2, :heads] = decay_ref[...]
        small[...] = jnp.zeros_like(small)
        small[7:8, :heads] = skip_ref[...]
        project()
        raw = dot(hx[:length], wdt_ref[...]).astype(BF16).astype(F32)
        lane = iota((length, 128), 1)
        raw = jnp.where(lane < heads, raw + par[0:1, :], 0.0)
        step = jnp.maximum(raw, 0.0) + jnp.log1p(jnp.exp(-jnp.abs(raw)))
        step = jnp.where(lane < heads, step, 0.0)
        step_ref[...] = step
        rate = -step * par[1:2, :]
        lower = jnp.where(triangle(True), 1.0, 0.0)
        upper = jnp.where(triangle(False), 1.0, 0.0)
        live = iota((CHUNK, 128), 1) < heads
        before = jnp.zeros((1, 128), F32)
        backs, totals = [], []
        for c in range(chunks):
            rows = slice(c * CHUNK, (c + 1) * CHUNK)
            head = jnp.dot(lower, rate[rows], precision=HIGHEST, preferred_element_type=F32)
            tail = jnp.dot(upper, rate[rows], precision=HIGHEST, preferred_element_type=F32)
            total = head[CHUNK - 1 :]
            dt = step[rows]

            def put(ref, value):
                ref[rows, :] = high_low(jnp.where(live, value, 0.0), heads)

            put(wf, dt * jnp.exp(jnp.minimum(total - head, 0.0)))
            put(wb, dt * jnp.exp(jnp.minimum(total - tail, 0.0)))
            put(of, jnp.exp(jnp.minimum(head - total, 80.0)))
            put(ob, jnp.exp(jnp.minimum(tail - total, 80.0)))
            put(ef_ref, jnp.exp(head + before))
            before = before + total
            backs.append(tail)
            totals.append(total)
            tot_ref[c : c + 1, :] = total
            small[c : c + 1, :] = jnp.exp(total)
            span_ref[c] = -jnp.min(total)
        tot_ref[chunks:, :] = jnp.zeros((8 - chunks, 128), F32)
        small[6:7, :] = before
        after = jnp.zeros((1, 128), F32)
        for c in reversed(range(chunks)):
            rows = slice(c * CHUNK, (c + 1) * CHUNK)
            eb_ref[rows, :] = high_low(jnp.where(live, jnp.exp(backs[c] + after), 0.0), heads)
            after = after + totals[c]
        for c in range(chunks):
            rows = slice(c * CHUNK, (c + 1) * CHUNK)
            forward, backward = convolved(c)
            for value, out, gc, bt, keep in (
                (forward, xf_ref, gcf, btf, triangle(True)),
                (backward, xb_ref, gcb, btb, triangle(False)),
            ):
                rounded = value.astype(BF16)
                out[rows, :] = rounded
                b_part, c_part = rounded[:, :state], rounded[:, state:]
                gc[rows, :CHUNK] = jnp.where(keep, dot_nt(c_part, b_part), 0.0).astype(BF16)
                gc[rows, CHUNK:] = c_part
                bt[rows, :] = value[:, :state].T.astype(BF16)

    @pl.when((j > 0) & (j <= tiles))
    def _():
        project()
        first = (j - 1) * (TILE // head_dim)
        spread = spread_matrix(first, heads, head_dim, 2).astype(BF16)
        rows8 = jnp.dot(
            small[...], spread_matrix(first, heads, head_dim, 1), precision=HIGHEST, preferred_element_type=F32
        )
        skip = rows8[7:8]
        weighted_b, y_base = [], []
        running = jnp.zeros((state, TILE), F32)
        for c in range(chunks):
            rows = slice(c * CHUNK, (c + 1) * CHUNK)
            forward, backward = convolved(c)
            xf_ref[rows, :] = forward.astype(BF16)
            xb_ref[rows, :] = backward.astype(BF16)
            scaled = (forward * dot(wf[rows, :], spread)).astype(BF16)
            decayed = running * rows8[c : c + 1]
            sf_ref[c] = running.astype(BF16)
            mixed = dot(gcf[rows, :], jnp.concatenate([scaled, decayed.astype(BF16)], 0))
            yf_ref[rows, :] = (mixed * dot(of[rows, :], spread) + skip * forward).astype(BF16)
            running = decayed + dot(btf[rows, :], scaled)
        ends = [running]
        running = jnp.zeros((state, TILE), F32)
        for c in reversed(range(chunks)):
            rows = slice(c * CHUNK, (c + 1) * CHUNK)
            backward = xb_ref[rows, :].astype(F32)
            scaled = (backward * dot(wb[rows, :], spread)).astype(BF16)
            decayed = running * rows8[c : c + 1]
            sb_ref[c] = running.astype(BF16)
            mixed = dot(gcb[rows, :], jnp.concatenate([scaled, decayed.astype(BF16)], 0))
            yb_ref[rows, :] = (mixed * dot(ob[rows, :], spread) + skip * backward).astype(BF16)
            running = decayed + dot(btb[rows, :], scaled)
        ends.append(running)
        total = rows8[6:7]
        high = total.astype(BF16).astype(F32)
        middle = (total - high).astype(BF16).astype(F32)
        low = total - high - middle
        extra = jnp.concatenate([high, middle, low, jnp.zeros((13, TILE), F32)], 0).astype(BF16)
        for strand in range(2):
            for half in range(TILE // 128):
                lanes = slice(half * 128, (half + 1) * 128)
                end_ref[half, strand, :state, :] = ends[strand][:, lanes].astype(BF16)
                end_ref[half, strand, state:, :] = extra[:, lanes]

    @pl.when(j > tiles)
    def _():
        gate_ref[...] = dot(x_ref[...], w_ref[...]).astype(BF16)


def carry_kernel(end_ref, in_ref, arrived, answers, out_sem, in_sem, out_sem2, in_sem2, own_sem):
    count = end_ref.shape[0]
    state = in_ref.shape[2]
    me = lax.axis_index("ctx")
    barrier = pltpu.get_barrier_semaphore()
    peers = [lax.rem(me + d, count) for d in range(1, count)]
    for peer in peers:
        pl.semaphore_signal(barrier, inc=1, device_id={"ctx": peer}, device_id_type=MESH)
    pl.semaphore_wait(barrier, count - 1)

    def send(src, dst, sems, sem_to, peer):
        return pltpu.make_async_remote_copy(
            src_ref=src, dst_ref=dst, send_sem=sems, recv_sem=sem_to, device_id={"ctx": peer}, device_id_type=MESH
        )

    first = [send(end_ref.at[p], arrived.at[me], out_sem.at[p], in_sem.at[me], p) for p in peers]
    for copy in first:
        copy.start()
    own = pltpu.make_async_copy(end_ref.at[me], arrived.at[me], own_sem.at[0])
    own.start()
    own.wait()
    for p in peers:
        send(end_ref.at[p], arrived.at[p], out_sem.at[p], in_sem.at[p], p).wait_recv()

    def factor(k):
        rows = arrived[k, 0, state : state + 16, :].astype(F32)
        return jnp.exp(rows[0:1] + rows[1:2] + rows[2:3])

    running = jnp.zeros((state, 128), F32)
    for k in range(count):
        answers[k, 0] = running.astype(BF16)
        if k < count - 1:
            running = factor(k) * running + arrived[k, 0, :state, :].astype(F32)
    running = jnp.zeros((state, 128), F32)
    for k in reversed(range(count)):
        answers[k, 1] = running.astype(BF16)
        if k > 0:
            running = factor(k) * running + arrived[k, 1, :state, :].astype(F32)
    second = [send(answers.at[p], in_ref.at[me], out_sem2.at[p], in_sem2.at[me], p) for p in peers]
    for copy in second:
        copy.start()
    own = pltpu.make_async_copy(answers.at[me], in_ref.at[me], own_sem.at[1])
    own.start()
    own.wait()
    for p in peers:
        send(answers.at[p], in_ref.at[p], out_sem2.at[p], in_sem2.at[p], p).wait_recv()
    for copy in first:
        copy.wait_send()
    for copy in second:
        copy.wait_send()


def back_kernel(
    heads, head_dim, state, inner, span_ref, yf_ref, yb_ref, gate_ref, cf_ref, cb_ref, ef_ref, eb_ref, in_ref, x_ref,
    w_ref, gain_ref, decay_ref, skip_ref, tot_ref, xf_any, xb_any, sf_any, sb_any, step_any,
    out_ref, gf, gb, accf, accb, normed, par, xbuf, sbuf, dtbuf, sem,
):
    rows = out_ref.shape[0]
    i = pl.program_id(0)
    per_block = rows // CHUNK
    worst = span_ref[i * per_block]
    for k in range(1, per_block):
        worst = jnp.maximum(worst, span_ref[i * per_block + k])

    @pl.when(worst <= LIMIT)
    def _():
        total_f = jnp.zeros((rows, 128), F32)
        total_b = jnp.zeros((rows, 128), F32)
        for j in range(inner // TILE):
            lanes = slice(j * TILE, (j + 1) * TILE)
            spread = spread_matrix(j * (TILE // head_dim), heads, head_dim, 2).astype(BF16)
            gate = silu(gate_ref[:, lanes].astype(F32))

            def strand(y_ref, c_ref, e_ref, s, g):
                entering = jnp.concatenate([in_ref[2 * j, s], in_ref[2 * j + 1, s]], 1)
                y = y_ref[:, lanes].astype(F32) + dot(e_ref[...], spread) * dot(c_ref[...], entering)
                y = y * gate
                g[:, lanes] = y
                square = y * y
                return square[:, :128] + square[:, 128:]

            total_f = total_f + strand(yf_ref, cf_ref, ef_ref, 0, gf)
            total_b = total_b + strand(yb_ref, cb_ref, eb_ref, 1, gb)
        accf[...] = total_f
        accb[...] = total_b

    @pl.when(jnp.logical_not(worst <= LIMIT))
    def _():
        par[...] = jnp.zeros_like(par)
        par[0:1, :heads] = decay_ref[...]
        par[1:2, :heads] = skip_ref[...]
        accf[...] = jnp.zeros_like(accf)
        accb[...] = jnp.zeros_like(accb)
        for s, (x_any, s_any, g, acc) in enumerate(((xf_any, sf_any, gf, accf), (xb_any, sb_any, gb, accb))):
            keep = triangle(s == 0)
            ones = jnp.where(keep, 1.0, 0.0)

            def one_chunk(k, _):
                c = i * per_block + k
                copies = [
                    pltpu.make_async_copy(x_any.at[pl.ds(c * CHUNK, CHUNK)], xbuf, sem.at[0]),
                    pltpu.make_async_copy(s_any.at[c], sbuf, sem.at[1]),
                    pltpu.make_async_copy(step_any.at[pl.ds(c * CHUNK, CHUNK)], dtbuf, sem.at[2]),
                ]
                for copy in copies:
                    copy.start()
                for copy in copies:
                    copy.wait()
                at = pl.ds(pl.multiple_of(k * CHUNK, CHUNK), CHUNK)
                dt = dtbuf[...]
                log_decay = jnp.dot(ones, -dt * par[0:1, :], precision=HIGHEST, preferred_element_type=F32)
                number = iota((8, 128), 0)
                counted = (number < c) if s == 0 else (number > c)
                offset = jnp.sum(jnp.where(counted, tot_ref[...], 0.0), 0, keepdims=True)
                log_t, dt_t = log_decay.T, dt.T
                b_part, c_part = xbuf[:, inner : inner + state], xbuf[:, inner + state :]
                scores = dot_nt(c_part, b_part)
                lane, sub = iota((CHUNK, 128), 1), iota((128, CHUNK), 0)
                lane1 = iota((1, 128), 1)
                left = lane < head_dim

                def pair(q, _):
                    cols = pl.ds(pl.multiple_of(q * 128, 128), 128)
                    v = xbuf[:, cols]
                    outs, ups, skips, offsets = [], [], [], []
                    for half in range(2):
                        h = 2 * q + half
                        column = jnp.sum(jnp.where(lane == h, log_decay, 0.0), 1, keepdims=True)
                        line = jnp.sum(jnp.where(sub == h, log_t, 0.0), 0, keepdims=True)
                        dt_line = jnp.sum(jnp.where(sub == h, dt_t, 0.0), 0, keepdims=True)
                        decay = jnp.where(keep, jnp.exp(jnp.minimum(column - line, 0.0)), 0.0)
                        outs.append(dot((decay * scores * dt_line).astype(BF16), v))
                        ups.append(jnp.exp(column))
                        skips.append(jnp.sum(jnp.where(lane1 == h, par[1:2, :], 0.0), 1, keepdims=True))
                        offsets.append(jnp.sum(jnp.where(lane1 == h, offset, 0.0), 1, keepdims=True))
                    shift = jnp.where(lane1 < head_dim, offsets[0], offsets[1])
                    entering = sbuf[:, cols].astype(F32) + jnp.exp(shift) * in_ref[q, s].astype(F32)
                    carried = dot(c_part, entering.astype(BF16))
                    y = jnp.where(left, outs[0], outs[1]) + jnp.where(left, ups[0], ups[1]) * carried
                    y = y + jnp.where(lane1 < head_dim, skips[0], skips[1]) * v.astype(F32)
                    y = y * silu(gate_ref[at, cols].astype(F32))
                    g[at, cols] = y
                    acc[at, :] += y * y
                    return 0

                lax.fori_loop(0, heads // 2, pair, 0)
                return 0

            lax.fori_loop(0, per_block, one_chunk, 0)

    scale_f = lax.rsqrt(jnp.sum(accf[...], 1, keepdims=True) * (1.0 / inner) + 1e-05)
    scale_b = lax.rsqrt(jnp.sum(accb[...], 1, keepdims=True) * (1.0 / inner) + 1e-05)
    for j in range(inner // TILE):
        lanes = slice(j * TILE, (j + 1) * TILE)
        value = (gf[:, lanes] * scale_f + gb[:, lanes] * scale_b) * gain_ref[:, lanes]
        normed[:, lanes] = value.astype(BF16)
    out_ref[...] = (x_ref[...].astype(F32) + dot(normed[...], w_ref[...])).astype(BF16)


def local(hidden, in_weight, conv_weight, conv_bias, step_bias, decay_rate, skip_gain, norm_gain, out_weight):
    length, width = hidden.shape
    heads = step_bias.shape[0]
    inner = out_weight.shape[0]
    head_dim = inner // heads
    conv_width = conv_weight.shape[1]
    state = (conv_width - inner) // 2
    chunks = length // CHUNK
    tiles = inner // TILE
    count = lax.axis_size("ctx")
    ring = range(count)
    prev = lax.ppermute(hidden[length - HALO :], "ctx", [(i, i + 1) for i in ring if i + 1 < count])
    follow = lax.ppermute(hidden[:HALO], "ctx", [(i + 1, i) for i in ring if i + 1 < count])
    sizes = (heads, head_dim, state, inner)

    def whole(shape, **kw):
        return pl.BlockSpec(shape, lambda j: (0,) * len(shape), **kw)

    def value_tile(j):
        return jnp.clip(j - 1, 0, tiles - 1)

    def conv_tile(j):
        return jnp.where(j == 0, tiles, value_tile(j))

    def weight_tile(j):
        return jnp.where(j == 0, 2 * tiles, jnp.where(j <= tiles, tiles - 1 + j, j - tiles - 1))

    def shape(dims, dtype):
        return jax.ShapeDtypeStruct(dims, dtype)

    row2 = lambda a: a.reshape(1, -1)
    once = dict(pipeline_mode=pl.Buffered(1))
    outs = pl.pallas_call(
        functools.partial(front_kernel, *sizes),
        name="front",
        grid=(1 + 2 * tiles,),
        in_specs=[
            whole((length, width), **once),
            whole((HALO, width)),
            whole((HALO, width)),
            pl.BlockSpec((width, TILE), lambda j: (0, weight_tile(j))),
            pl.BlockSpec((width, 128), lambda j: (0, (inner + conv_width) // 128), **once),
            pl.BlockSpec((4, TILE), lambda j: (0, conv_tile(j))),
            pl.BlockSpec((1, TILE), lambda j: (0, conv_tile(j))),
            whole((1, heads)),
            whole((1, heads)),
            whole((1, heads)),
        ],
        out_specs=[
            pl.BlockSpec((length, TILE), lambda j: (0, jnp.maximum(j - tiles - 1, 0))),
            pl.BlockSpec((length, TILE), lambda j: (0, conv_tile(j))),
            pl.BlockSpec((length, TILE), lambda j: (0, conv_tile(j))),
            pl.BlockSpec((length, TILE), lambda j: (0, value_tile(j))),
            pl.BlockSpec((length, TILE), lambda j: (0, value_tile(j))),
            pl.BlockSpec((chunks, state, TILE), lambda j: (0, 0, value_tile(j))),
            pl.BlockSpec((chunks, state, TILE), lambda j: (0, 0, value_tile(j))),
            pl.BlockSpec((TILE // 128, 2, state + 16, 128), lambda j: (value_tile(j), 0, 0, 0)),
            whole((length, 128)),
            whole((length, 128)),
            whole((length, 128)),
            whole((8, 128)),
            pl.BlockSpec(memory_space=pltpu.SMEM),
        ],
        out_shape=[
            shape((length, inner), BF16),
            shape((length, conv_width), BF16),
            shape((length, conv_width), BF16),
            shape((length, inner), BF16),
            shape((length, inner), BF16),
            shape((chunks, state, inner), BF16),
            shape((chunks, state, inner), BF16),
            shape((inner // 128, 2, state + 16, 128), BF16),
            shape((length, 128), BF16),
            shape((length, 128), BF16),
            shape((length, 128), F32),
            shape((8, 128), F32),
            shape((8,), F32),
        ],
        scratch_shapes=[
            pltpu.VMEM((length + 2 * HALO, width), BF16),
            pltpu.VMEM((length + 2 * HALO, TILE), F32),
            pltpu.VMEM((8, 128), F32),
        ]
        + [pltpu.VMEM((length, 128), BF16)] * 4
        + [pltpu.VMEM((length, CHUNK + state), BF16)] * 2
        + [pltpu.VMEM((chunks * state, CHUNK), BF16)] * 2
        + [pltpu.VMEM((8, 128), F32)],
        compiler_params=pltpu.CompilerParams(vmem_limit_bytes=48 << 20),
    )(
        hidden, follow, prev, in_weight, in_weight, conv_weight, row2(conv_bias), row2(step_bias), row2(decay_rate),
        row2(skip_gain),
    )
    gate, xf, xb, yf, yb, sf, sb, end, ef, eb, step, tot, span = outs
    entering = pl.pallas_call(
        carry_kernel,
        name="carry",
        in_specs=[pl.BlockSpec(memory_space=pltpu.VMEM)],
        out_specs=pl.BlockSpec(memory_space=pltpu.VMEM),
        out_shape=shape((count, 2, state, 128), BF16),
        scratch_shapes=[
            pltpu.VMEM((count, 2, state + 16, 128), BF16),
            pltpu.VMEM((count, 2, state, 128), BF16),
            pltpu.SemaphoreType.DMA((count,)),
            pltpu.SemaphoreType.DMA((count,)),
            pltpu.SemaphoreType.DMA((count,)),
            pltpu.SemaphoreType.DMA((count,)),
            pltpu.SemaphoreType.DMA((2,)),
        ],
        compiler_params=pltpu.CompilerParams(collective_id=0, has_side_effects=True),
    )(end)
    anywhere = pl.BlockSpec(memory_space=pl.ANY)
    block = pl.BlockSpec((ROWS, inner), lambda j: (j, 0))
    c_block = pl.BlockSpec((ROWS, state), lambda j: (j, inner // state + 1))
    e_block = pl.BlockSpec((ROWS, 128), lambda j: (j, 0))
    return pl.pallas_call(
        functools.partial(back_kernel, *sizes),
        name="back",
        grid=(length // ROWS,),
        in_specs=[
            pl.BlockSpec(memory_space=pltpu.SMEM),
            block, block, block, c_block, c_block, e_block, e_block,
            whole((count, 2, state, 128), **once),
            pl.BlockSpec((ROWS, width), lambda j: (j, 0)),
            whole((inner, width), **once),
            whole((1, inner)),
            whole((1, heads)),
            whole((1, heads)),
            whole((8, 128)),
        ]
        + [anywhere] * 5,
        out_specs=pl.BlockSpec((ROWS, width), lambda j: (j, 0)),
        out_shape=shape((length, width), BF16),
        scratch_shapes=[
            pltpu.VMEM((ROWS, inner), F32),
            pltpu.VMEM((ROWS, inner), F32),
            pltpu.VMEM((ROWS, 128), F32),
            pltpu.VMEM((ROWS, 128), F32),
            pltpu.VMEM((ROWS, inner), BF16),
            pltpu.VMEM((8, 128), F32),
            pltpu.VMEM((CHUNK, conv_width), BF16),
            pltpu.VMEM((state, inner), BF16),
            pltpu.VMEM((CHUNK, 128), F32),
            pltpu.SemaphoreType.DMA((3,)),
        ],
        compiler_params=pltpu.CompilerParams(vmem_limit_bytes=56 << 20),
    )(
        span, yf, yb, gate, xf, xb, ef, eb, entering, hidden, out_weight, row2(norm_gain), row2(decay_rate),
        row2(skip_gain), tot, xf, xb, sf, sb, step,
    )


def solution(mesh):
    return jax.shard_map(
        local,
        mesh=mesh,
        in_specs=(P(("dp", "ctx"), None), P(), P(), P(), P(), P(), P(), P(), P()),
        out_specs=P(("dp", "ctx"), None),
        check_vma=False,
    )
```

time: 567 us -> 124 us (0.22)
  the two profiles are of different devices: /device:TPU:0 before, /device:TPU:1 now
where the time goes in v1:
time: 124 us
  Pallas kernels  99 us (80%)
  local copies, waits for them, and re-layouts  17.7 us (14%)
  starting transfers between devices  6.83 us (6%)
    pallas_call x1, Pallas kernels, local(): pl.pallas_call(functools.partial(front_kernel, *sizes), name='front', gri...  46.9 us
    pallas_call x1, Pallas kernels, local(): pl.pallas_call(carry_kernel, name='carry', in_specs=[pl.BlockSpec(memory_...  39 us
    unnamed x23, local copies, waits for them, and re-layouts  16.3 us
    pallas_call x1, Pallas kernels, local(): pl.pallas_call(functools.partial(back_kernel, *sizes), name='back', grid=...  13.1 us
    ppermute x1, starting transfers between devices, local(): lax.ppermute(hidden[length - HALO:], 'ctx', [(i, i + 1) for i in ring if...  4.91 us
  transfers between devices with their start and end apart: 2, of which 0 were waited for; matrix products, arithmetic and copies ran while one was open for 10% of the time, Pallas kernels for 0%

profile of v1, /device:TPU:1, one launch (start us, length us, event | category | flops | bytes accessed | tf_op | source)
XLA Modules:
  0.0 123.7 jit_solution(9417747915238420330)
XLA Ops:
  0.0 0.7 fusion
  0.7 4.9 %collective-permute-start.1 = (bf16[8,1024]{1,0:T(8,128)(2,1)S(1)}, bf16[8,1024]{1,0:T(8,128)(2,1)S(1)}, u32[]{:S(2)}, u32[]{:S(2)}) collective-permute-start(bf16[8,1024]{1,0:T(8,128)(2,1)S(1)} %get-tuple-element.31), channel_id=1, source_target_pairs={{0,8},{8,16},{16,24},{24,32},{32,40},{40,48},{48,56},{56,64},{64,7... | collective-permute-start | bytes 49160 | tf_op jit(solution)/shard_map/ppermute | solution.py:369
  5.7 1.9 %collective-permute-start = (bf16[8,1024]{1,0:T(8,128)(2,1)S(1)}, bf16[8,1024]{1,0:T(8,128)(2,1)S(1)}, u32[]{:S(2)}, u32[]{:S(2)}) collective-permute-start(bf16[8,1024]{1,0:T(8,128)(2,1)S(1)} %get-tuple-element.32), channel_id=1, source_target_pairs={{8,0},{16,8},{24,16},{32,24},{40,32},{48,40},{56,48},{64,56},{72,6... | collective-permute-start | bytes 49160 | tf_op jit(solution)/shard_map/ppermute | solution.py:370
  7.6 0.7 reshape.17.cb_ref
  8.3 0.0 copy-start
  8.3 0.0 copy-start.5
  8.3 0.0 copy-start.7
  8.3 0.0 copy-start.8
  8.3 0.0 copy-start.9
  8.4 12.0 %copy.10.w_ref.wdt_ref = bf16[1024,4384]{1,0:T(8,128)(2,1)} copy(bf16[1024,4384]{0,1:T(8,128)(2,1)} %param.10) | data formatting | bytes 17956864 | tf_op args[1]
  20.4 0.0 collective-permute-done.1.prev_ref
  20.4 0.0 collective-permute-done.next_ref
  20.4 0.0 copy-done
  20.4 0.0 copy-done.5
  20.4 0.0 copy-done.7
  20.4 0.0 copy-done.8
  20.4 0.0 copy-done.9
  20.4 46.9 %front.1 = (bf16[768,2048]{1,0:T(8,128)(2,1)}, bf16[768,2304]{1,0:T(8,128)(2,1)}, bf16[768,2304]{1,0:T(8,128)(2,1)}, bf16[768,2048]{1,0:T(8,128)(2,1)}, bf16[768...) custom-call(bf16[768,1024]{1,0:T(8,128)(2,1)S(1)} %copy-done, ...), custom_call_target="tpu_custom_call" | custom-call | tf_op jit(solution)/shard_map/front/pallas_call | solution.py:390
  67.3 0.0 copy-start.1
  67.3 1.0 copy-done.1
  68.3 0.0 copy-start.2
  68.3 0.8 copy-done.2
  69.1 0.0 copy-start.3
  69.1 0.7 copy-done.3
  69.8 0.0 copy-start.4
  69.8 0.7 copy-done.4
  70.5 0.0 copy-start.6
  70.5 0.6 copy-done.6
  71.1 0.0 copy-start.10
  71.1 0.5 copy-done.10
  71.6 39.0 %carry.1.in_ref = bf16[16,2,128,128]{3,2,1,0:T(8,128)(2,1)} custom-call(bf16[16,2,144,128]{3,2,1,0:T(8,128)(2,1)} %copy-done.1), custom_call_target="tpu_custom_call" | custom-call | tf_op jit(solution)/shard_map/carry/pallas_call | solution.py:451
  110.6 13.1 %back.1 = bf16[768,1024]{1,0:T(8,128)(2,1)} custom-call(f32[8]{0:T(128)} %copy-done.10, bf16[768,2048]{1,0:T(8,128)(2,1)} %get-tuple-element.19.yf_ref, bf16[768,2048]{1,0:T(8,128)(2,1)} %get-tuple-element.20.yb_ref, bf16[768,2048]{1,0:T(8,128)(2,1)} %get-tuple-element.21.gate_ref, bf16[768,2304]{1,0:T(8,128)(2,1)} %get-tuple-element.22.cf_ref.xf_any, ...), custom_call_target="tpu_custom_call" | custom-call | tf_op jit(solution)/shard_map/back/pallas_call | solution.py:472
Async XLA Ops:
  0.7 19.6 %collective-permute-start.1 = (bf16[8,1024]{1,0:T(8,128)(2,1)S(1)}, bf16[8,1024]{1,0:T(8,128)(2,1)S(1)}, u32[]{:S(2)}, u32[]{:S(2)}) collective-permute-start(bf16[8,1024]{1,0:T(8,128)(2,1)S(1)} %get-tuple-element.31), channel_id=1, source_target_pairs={{0,8},{8,16},{16,24},{24,32},{32,40},{40,48},{48,56},{56,64},{64,7... | collective-permute-start | bytes 49160 | tf_op jit(solution)/shard_map/ppermute | solution.py:369
  5.7 14.7 %collective-permute-start = (bf16[8,1024]{1,0:T(8,128)(2,1)S(1)}, bf16[8,1024]{1,0:T(8,128)(2,1)S(1)}, u32[]{:S(2)}, u32[]{:S(2)}) collective-permute-start(bf16[8,1024]{1,0:T(8,128)(2,1)S(1)} %get-tuple-element.32), channel_id=1, source_target_pairs={{8,0},{16,8},{24,16},{32,24},{40,32},{48,40},{56,48},{64,56},{72,6... | collective-permute-start | bytes 49160 | tf_op jit(solution)/shard_map/ppermute | solution.py:370
  8.3 12.1 %copy-start = (bf16[768,1024]{1,0:T(8,128)(2,1)S(1)}, bf16[768,1024]{1,0:T(8,128)(2,1)}, u32[]{:S(2)}) copy-start(bf16[768,1024]{1,0:T(8,128)(2,1)} %x_ref.3) | copy-start | bytes 4718596
  8.3 12.1 %copy-start.5 = (f32[4,2304]{1,0:T(4,128)S(1)}, f32[4,2304]{1,0:T(4,128)}, u32[]{:S(2)}) copy-start(f32[4,2304]{1,0:T(4,128)} %cw_ref.1) | copy-start | bytes 110596
  8.3 12.1 %copy-start.7 = (f32[32]{0:T(128)S(1)}, f32[32]{0:T(128)}, u32[]{:S(2)}) copy-start(f32[32]{0:T(128)} %param.14) | copy-start | bytes 388
  8.3 12.1 %copy-start.8 = (f32[32]{0:T(128)S(1)}, f32[32]{0:T(128)}, u32[]{:S(2)}) copy-start(f32[32]{0:T(128)} %param.15) | copy-start | bytes 388
  8.3 12.1 %copy-start.9 = (f32[32]{0:T(128)S(1)}, f32[32]{0:T(128)}, u32[]{:S(2)}) copy-start(f32[32]{0:T(128)} %param.13) | copy-start | bytes 388
  67.3 1.0 copy-start.1
  68.3 0.8 copy-start.2
  69.1 0.7 copy-start.3
  69.8 0.7 copy-start.4
  70.5 0.6 copy-start.6
  71.1 0.5 copy-start.10

commit v2 on v1

v2 whole, which is shorter than its diff:
```python
import functools

import jax
import jax.numpy as jnp
from jax import lax
from jax.experimental import pallas as pl
from jax.experimental.pallas import tpu as pltpu
from jax.sharding import PartitionSpec as P

CHUNK = 128
TILE = 256
HALO = 8
ROWS = 256
LIMIT = 40.0
VMEM = 66_000_000
MESH = pl.DeviceIdType.MESH
HIGHEST = lax.Precision.HIGHEST
F32 = jnp.float32
BF16 = jnp.bfloat16


def dot(a, b):
    return jnp.dot(a, b, preferred_element_type=F32)


def dot_nt(a, b):
    return lax.dot_general(a, b, (((1,), (1,)), ((), ())), preferred_element_type=F32)


def silu(x):
    half = 0.5 * x
    return half + half * jnp.tanh(half)


def iota(shape, dim):
    return lax.broadcasted_iota(jnp.int32, shape, dim)


def iota_mod(shape, dim, mod):
    return lax.rem(iota(shape, dim), mod)


def time_of(index):
    return lax.rem(index, 8) * (CHUNK // 8) + lax.div(index, 8)


def triangle(lower):
    row, column = time_of(iota((CHUNK, CHUNK), 0)), time_of(iota((CHUNK, CHUNK), 1))
    return row >= column if lower else row <= column


def shuffle(inverse):
    row, column = iota((CHUNK, CHUNK), 0), iota((CHUNK, CHUNK), 1)
    hit = row == time_of(column) if inverse else time_of(row) == column
    return jnp.where(hit, 1.0, 0.0).astype(BF16)


def high_low(x):
    high = x.astype(BF16)
    return jnp.concatenate([high, (x - high.astype(F32)).astype(BF16)], 1)


def three_terms(x):
    high = x.astype(BF16).astype(F32)
    middle = (x - high).astype(BF16).astype(F32)
    return [high, middle, x - high - middle]


def spread_matrix(first, head_dim, depth):
    row, column = iota_mod((depth, TILE), 0, 128), iota((depth, TILE), 1)
    return jnp.where(row == first + lax.div(column, head_dim), 1.0, 0.0).astype(BF16)


def front_kernel(
    heads, head_dim, state, inner, x_ref, next_ref, prev_ref, w_ref, wdt_ref, cw_ref, cb_ref, bias_ref, decay_ref, skip_ref,
    gate_ref, xf_ref, xb_ref, yf_ref, yb_ref, sf_ref, sb_ref, end_ref, ef_ref, eb_ref, step_ref, off_ref, span_ref,
    hx, xs, par, wf, wb, of, ob, gcf, gcb, btf, btb, small, rhsf, rhsb,
):
    length = x_ref.shape[0]
    chunks = length // CHUNK
    tiles = inner // TILE
    packs = 128 // heads
    groups = off_ref.shape[0] // 4
    edge = 24
    span = CHUNK + 2 * edge
    j = pl.program_id(0)

    def project():
        out = dot_nt(hx[...], w_ref[...])
        for c in range(chunks):
            xs[c * span + edge : c * span + edge + CHUNK] = out[c * CHUNK : (c + 1) * CHUNK]
        sub = iota((8, TILE), 0)

        def rolled(c, r, by):
            at = c * span + edge + r * 8
            return pltpu.roll(xs[at : at + 8], by, 0)

        for p in range(3):
            r = CHUNK // 8 - 3 + p
            before = jnp.broadcast_to(out[length + 2 * HALO - 3 + p : length + 2 * HALO - 2 + p], (8, TILE))
            for c in range(chunks):
                mine = rolled(c, r, 1)
                xs[c * span + p * 8 : c * span + p * 8 + 8] = jnp.where(sub == 0, before, mine)
                before = mine
            after = jnp.broadcast_to(out[length + p : length + p + 1], (8, TILE))
            for c in reversed(range(chunks)):
                mine = rolled(c, p, 7)
                at = c * span + edge + CHUNK + p * 8
                xs[at : at + 8] = jnp.where(sub == 7, after, mine)
                after = mine

    def convolved(c):
        at = c * span + edge
        taps = [cw_ref[k : k + 1, :] for k in range(4)]
        base = xs[at : at + CHUNK] * taps[3] + cb_ref[...]
        forward, backward = base, base
        for k in range(1, 4):
            forward = forward + xs[at - 8 * k : at - 8 * k + CHUNK] * taps[3 - k]
            backward = backward + xs[at + 8 * k : at + 8 * k + CHUNK] * taps[3 - k]
        return silu(forward), silu(backward)

    @pl.when(j == 0)
    def _():
        order = shuffle(False)
        for c in range(chunks):
            rows = slice(c * CHUNK, (c + 1) * CHUNK)
            hx[rows] = dot(order, x_ref[rows]).astype(BF16)
        hx[length:] = jnp.concatenate(
            [next_ref[...].astype(F32), prev_ref[...].astype(F32)], 0
        ).astype(BF16)
        par[...] = jnp.zeros_like(par)
        for q in range(packs):
            par[0:1, q * heads : (q + 1) * heads] = bias_ref[...]
            par[1:2, q * heads : (q + 1) * heads] = decay_ref[...]
        par[2:3, :heads] = skip_ref[...]
        project()
        lower = jnp.where(triangle(True), 1.0, 0.0)
        upper = jnp.where(triangle(False), 1.0, 0.0)
        lane1 = iota((1, 128), 1)
        wdt = wdt_ref[...]
        zero = jnp.zeros((128, wdt.shape[1]), BF16)
        totals, kept = [], []
        for g in range(groups):
            members = range(g * packs, min((g + 1) * packs, chunks))
            raw = jnp.zeros((CHUNK, 128), F32)
            for q, c in enumerate(members):
                parts = [zero[: q * heads], wdt, zero[: 128 - (q + 1) * heads]]
                wide = jnp.concatenate([p for p in parts if p.shape[0]], 0)
                raw = raw + dot_nt(hx[c * CHUNK : (c + 1) * CHUNK], wide)
            raw = raw.astype(BF16).astype(F32) + par[0:1, :]
            step = jnp.maximum(raw, 0.0) + jnp.log1p(jnp.exp(-jnp.abs(raw)))
            step = jnp.where(iota((CHUNK, 128), 1) < len(members) * heads, step, 0.0)
            step_ref[g] = step
            rate = -step * par[1:2, :]
            head = jnp.dot(lower, rate, precision=HIGHEST, preferred_element_type=F32)
            tail = jnp.dot(upper, rate, precision=HIGHEST, preferred_element_type=F32)
            total = head[CHUNK - 1 :]
            wf[g] = high_low(step * jnp.exp(jnp.minimum(total - head, 0.0)))
            wb[g] = high_low(step * jnp.exp(jnp.minimum(total - tail, 0.0)))
            of[g] = high_low(jnp.exp(jnp.minimum(head - total, 80.0)))
            ob[g] = high_low(jnp.exp(jnp.minimum(tail - total, 80.0)))
            totals.append(total)
            kept.append((head, tail))
            span_ref[g] = -jnp.min(total)

        def wide8(x):
            return jnp.broadcast_to(x, (8, 128))

        def both(x):
            w = wide8(x)
            for q in range(1, packs):
                w = w + pltpu.roll(wide8(x), q * heads, 1)
            return w[0:1]

        lane8 = iota((8, 128), 1)
        sums = [both(t) for t in totals]
        slab = sums[0]
        for t in sums[1:]:
            slab = slab + t
        for g in range(groups):
            t8 = wide8(totals[g])
            early, late = jnp.zeros((8, 128), F32), jnp.zeros((8, 128), F32)
            for q in range(1, packs):
                early = early + jnp.where(lane8 >= q * heads, pltpu.roll(t8, q * heads, 1), 0.0)
                late = late + jnp.where(lane8 < 128 - q * heads, pltpu.roll(t8, 128 - q * heads, 1), 0.0)
            early, late = early[0:1], late[0:1]
            for k in range(groups):
                if k < g:
                    early = early + sums[k]
                if k > g:
                    late = late + sums[k]
            off_ref[g : g + 1, :] = early
            off_ref[groups + g : groups + g + 1, :] = late
            off_ref[2 * groups + 2 * g : 2 * groups + 2 * g + 2, :] = jnp.zeros((2, 128), F32)
            ef_ref[g] = high_low(jnp.exp(kept[g][0] + early))
            eb_ref[g] = high_low(jnp.exp(kept[g][1] + late))
        lines = []
        for g in range(groups):
            lines += three_terms(jnp.exp(totals[g]))
        lines += three_terms(slab) + three_terms(par[2:3, :])
        lines.append(jnp.zeros((16 - len(lines), 128), F32))
        small[...] = jnp.concatenate(lines, 0).astype(BF16)
        for c in range(chunks):
            rows = slice(c * CHUNK, (c + 1) * CHUNK)
            forward, backward = convolved(c)
            for value, out, gc, bt, keep in (
                (forward, xf_ref, gcf, btf, triangle(True)),
                (backward, xb_ref, gcb, btb, triangle(False)),
            ):
                rounded = value.astype(BF16)
                out[rows, :] = rounded
                b_part, c_part = rounded[:, :state], rounded[:, state:]
                gc[rows, :CHUNK] = jnp.where(keep, dot_nt(c_part, b_part), 0.0).astype(BF16)
                gc[rows, CHUNK:] = c_part
                bt[rows, :] = value[:, :state].T.astype(BF16)

    @pl.when((j > 0) & (j <= tiles))
    def _():
        project()
        first = (j - 1) * (TILE // head_dim)
        spreads = [spread_matrix(first + q * heads, head_dim, 256) for q in range(packs)]
        lines = [dot(small[...], spread[:128]) for spread in spreads]

        def line(q, k):
            rows = lines[q][3 * k : 3 * k + 3]
            return rows[0:1] + rows[1:2] + rows[2:3]

        fade = [line(c % packs, c // packs) for c in range(chunks)]
        slab, skip = line(0, groups), line(0, groups + 1)
        for c in range(chunks):
            rows = slice(c * CHUNK, (c + 1) * CHUNK)
            g, spread = c // packs, spreads[c % packs]
            forward, backward = convolved(c)
            xf_ref[rows, :] = forward.astype(BF16)
            xb_ref[rows, :] = backward.astype(BF16)
            rhsf[c, :CHUNK] = (forward * dot(wf[g], spread)).astype(BF16)
            rhsb[c, :CHUNK] = (backward * dot(wb[g], spread)).astype(BF16)
        ends = []
        for order, s_ref, bt, rhs in (
            (range(chunks), sf_ref, btf, rhsf),
            (reversed(range(chunks)), sb_ref, btb, rhsb),
        ):
            running = jnp.zeros((state, TILE), F32)
            for c in order:
                rows = slice(c * CHUNK, (c + 1) * CHUNK)
                decayed = running * fade[c]
                s_ref[c] = running.astype(BF16)
                rhs[c, CHUNK:] = decayed.astype(BF16)
                running = decayed + dot(bt[rows, :], rhs[c, :CHUNK])
            ends.append(running)
        extra = jnp.concatenate(three_terms(slab) + [jnp.zeros((13, TILE), F32)], 0).astype(BF16)
        for strand in range(2):
            for half in range(TILE // 128):
                lanes = slice(half * 128, (half + 1) * 128)
                end_ref[half, strand, :state, :] = ends[strand][:, lanes].astype(BF16)
                end_ref[half, strand, state:, :] = extra[:, lanes]
        for c in range(chunks):
            rows = slice(c * CHUNK, (c + 1) * CHUNK)
            g, spread = c // packs, spreads[c % packs]
            for y_ref, x_out, gc, rhs, o in (
                (yf_ref, xf_ref, gcf, rhsf, of),
                (yb_ref, xb_ref, gcb, rhsb, ob),
            ):
                mixed = dot(gc[rows, :], rhs[c])
                y_ref[rows, :] = (mixed * dot(o[g], spread) + skip * x_out[rows, :].astype(F32)).astype(BF16)

    @pl.when(j > tiles)
    def _():
        gate_ref[...] = dot_nt(hx[:length], w_ref[...]).astype(BF16)


def carry_kernel(
    end_ref, in_ref, paired, chip, arrived, answers, entering, other, out_sem, in_sem, out_sem2, in_sem2, pair_out, pair_in,
    own_sem,
):
    pairs = end_ref.shape[0]
    state = in_ref.shape[2]
    count = pairs // 2
    me = lax.axis_index("ctx")
    core, mine = lax.rem(me, 2), lax.div(me, 2)
    partner = me + 1 - 2 * core
    barrier = pltpu.get_barrier_semaphore()
    chips = [lax.rem(mine + d, count) for d in range(1, count)]
    for peer in [partner] + [2 * k + core for k in chips]:
        pl.semaphore_signal(barrier, inc=1, device_id={"ctx": peer}, device_id_type=MESH)
    pl.semaphore_wait(barrier, count)

    def send(src, dst, sems, sem_to, peer):
        return pltpu.make_async_remote_copy(
            src_ref=src, dst_ref=dst, send_sem=sems, recv_sem=sem_to, device_id={"ctx": peer}, device_id_type=MESH
        )

    swap = send(
        end_ref.at[pl.ds((1 - core) * count, count)], paired, pair_out.at[0], pair_in.at[0], partner
    )
    swap.start()
    swap.wait()

    def total(ref, k):
        rows = ref[k, 0, state : state + 16, :].astype(F32)
        return rows[0:1] + rows[1:2] + rows[2:3]

    low = core == 0

    for k in range(count):
        at = core * count + k
        t_own, t_part = total(end_ref, at), total(paired, k)
        f_own, f_part = jnp.exp(t_own), jnp.exp(t_part)
        one = jnp.ones_like(f_own)
        own0, part0 = end_ref[at, 0, :state, :].astype(F32), paired[k, 0, :state, :].astype(F32)
        own1, part1 = end_ref[at, 1, :state, :].astype(F32), paired[k, 1, :state, :].astype(F32)
        ahead, behind = jnp.where(low, f_part, one), jnp.where(low, one, f_own)
        chip[k, 0, :state, :] = (own0 * ahead + part0 * behind).astype(BF16)
        ahead, behind = jnp.where(low, one, f_part), jnp.where(low, f_own, one)
        chip[k, 1, :state, :] = (own1 * ahead + part1 * behind).astype(BF16)
        extra = jnp.concatenate(three_terms(t_own + t_part) + [jnp.zeros((13, 128), F32)], 0).astype(BF16)
        chip[k, 0, state:, :] = extra
        chip[k, 1, state:, :] = extra
    first = [send(chip.at[k], arrived.at[mine], out_sem.at[k], in_sem.at[mine], 2 * k + core) for k in chips]
    for copy in first:
        copy.start()
    own = pltpu.make_async_copy(chip.at[mine], arrived.at[mine], own_sem.at[0])
    own.start()
    own.wait()
    for k in chips:
        send(chip.at[k], arrived.at[k], out_sem.at[k], in_sem.at[k], 2 * k + core).wait_recv()
    for strand, order in ((0, list(range(count))), (1, list(reversed(range(count))))):
        running = jnp.zeros((state, 128), F32)
        for k in order:
            answers[k, strand] = running.astype(BF16)
            if k != order[-1]:
                running = jnp.exp(total(arrived, k)) * running + arrived[k, strand, :state, :].astype(F32)
    second = [send(answers.at[k], entering.at[mine], out_sem2.at[k], in_sem2.at[mine], 2 * k + core) for k in chips]
    for copy in second:
        copy.start()
    own = pltpu.make_async_copy(answers.at[mine], entering.at[mine], own_sem.at[1])
    own.start()
    own.wait()
    for k in chips:
        send(answers.at[k], entering.at[k], out_sem2.at[k], in_sem2.at[k], 2 * k + core).wait_recv()
    for k in range(count):
        at = core * count + k
        f_own, f_part = jnp.exp(total(end_ref, at)), jnp.exp(total(paired, k))
        chip_f, chip_b = entering[k, 0].astype(F32), entering[k, 1].astype(F32)
        own_late_f = f_part * chip_f + paired[k, 0, :state, :].astype(F32)
        part_late_f = f_own * chip_f + end_ref[at, 0, :state, :].astype(F32)
        own_late_b = f_part * chip_b + paired[k, 1, :state, :].astype(F32)
        part_late_b = f_own * chip_b + end_ref[at, 1, :state, :].astype(F32)
        in_ref[at, 0] = jnp.where(low, chip_f, own_late_f).astype(BF16)
        other[k, 0] = jnp.where(low, part_late_f, chip_f).astype(BF16)
        in_ref[at, 1] = jnp.where(low, own_late_b, chip_b).astype(BF16)
        other[k, 1] = jnp.where(low, chip_b, part_late_b).astype(BF16)
    swap_back = send(other, in_ref.at[pl.ds(core * count, count)], pair_out.at[1], pair_in.at[1], partner)
    swap_back.start()
    swap_back.wait()
    for copy in first:
        copy.wait_send()
    for copy in second:
        copy.wait_send()


def back_kernel(
    heads, head_dim, state, inner, span_ref, yf_ref, yb_ref, gate_ref, cf_ref, cb_ref, ef_ref, eb_ref, in_ref, x_ref,
    w_ref, gain_ref, decay_ref, skip_ref, off_ref, xf_any, xb_any, sf_any, sb_any, step_any,
    out_ref, gf, gb, accf, accb, normed, par, xbuf, sbuf, dtbuf, sem,
):
    rows = out_ref.shape[0]
    i = pl.program_id(0)
    per_block = rows // CHUNK
    packs = 128 // heads
    groups = off_ref.shape[0] // 4
    group = lax.div(i * per_block, packs)
    slot = lax.rem(i * per_block, packs)
    worst = span_ref[group]

    @pl.when(worst <= LIMIT)
    def _():
        total_f = jnp.zeros((rows, 128), F32)
        total_b = jnp.zeros((rows, 128), F32)
        for j in range(inner // TILE):
            lanes = slice(j * TILE, (j + 1) * TILE)
            first = j * (TILE // head_dim)
            spreads = [spread_matrix(first + (slot + k) * heads, head_dim, 256) for k in range(per_block)]
            gate = silu(gate_ref[:, lanes].astype(F32))

            def strand(y_ref, c_ref, e_ref, s, g):
                entering = jnp.concatenate([in_ref[2 * j, s], in_ref[2 * j + 1, s]], 1)
                y = y_ref[:, lanes].astype(F32) + jnp.concatenate([dot(e_ref[0], s) for s in spreads], 0) * dot(
                    c_ref[...], entering
                )
                y = y * gate
                g[:, lanes] = y
                square = y * y
                return square[:, :128] + square[:, 128:]

            total_f = total_f + strand(yf_ref, cf_ref, ef_ref, 0, gf)
            total_b = total_b + strand(yb_ref, cb_ref, eb_ref, 1, gb)
        accf[...] = total_f
        accb[...] = total_b

    @pl.when(jnp.logical_not(worst <= LIMIT))
    def _():
        par[...] = jnp.zeros_like(par)
        for q in range(packs):
            par[0:1, q * heads : (q + 1) * heads] = decay_ref[...]
            par[1:2, q * heads : (q + 1) * heads] = skip_ref[...]
        accf[...] = jnp.zeros_like(accf)
        accb[...] = jnp.zeros_like(accb)
        for s, (x_any, s_any, g, acc) in enumerate(((xf_any, sf_any, gf, accf), (xb_any, sb_any, gb, accb))):
            keep = triangle(s == 0)
            ones = jnp.where(keep, 1.0, 0.0)

            def one_chunk(k, _):
                c = i * per_block + k
                copies = [
                    pltpu.make_async_copy(x_any.at[pl.ds(c * CHUNK, CHUNK)], xbuf, sem.at[0]),
                    pltpu.make_async_copy(s_any.at[c], sbuf, sem.at[1]),
                    pltpu.make_async_copy(step_any.at[group], dtbuf, sem.at[2]),
                ]
                for copy in copies:
                    copy.start()
                for copy in copies:
                    copy.wait()
                at = pl.ds(pl.multiple_of(k * CHUNK, CHUNK), CHUNK)
                dt = dtbuf[...]
                log_decay = jnp.dot(ones, -dt * par[0:1, :], precision=HIGHEST, preferred_element_type=F32)
                picked = iota(off_ref.shape, 0) == s * groups + group
                offset = jnp.sum(jnp.where(picked, off_ref[...], 0.0), 0, keepdims=True)
                log_t, dt_t = log_decay.T, dt.T
                b_part, c_part = xbuf[:, inner : inner + state], xbuf[:, inner + state :]
                scores = dot_nt(c_part, b_part)
                lane, sub = iota((CHUNK, 128), 1), iota((128, CHUNK), 0)
                lane1 = iota((1, 128), 1)
                left = lane < head_dim

                def pair(q, _):
                    cols = pl.ds(pl.multiple_of(q * 128, 128), 128)
                    v = xbuf[:, cols]
                    outs, ups, skips, offsets = [], [], [], []
                    for half in range(2):
                        h = 2 * q + half + (slot + k) * heads
                        column = jnp.sum(jnp.where(lane == h, log_decay, 0.0), 1, keepdims=True)
                        line = jnp.sum(jnp.where(sub == h, log_t, 0.0), 0, keepdims=True)
                        dt_line = jnp.sum(jnp.where(sub == h, dt_t, 0.0), 0, keepdims=True)
                        decay = jnp.where(keep, jnp.exp(jnp.minimum(column - line, 0.0)), 0.0)
                        outs.append(dot((decay * scores * dt_line).astype(BF16), v))
                        ups.append(jnp.exp(column))
                        skips.append(jnp.sum(jnp.where(lane1 == h, par[1:2, :], 0.0), 1, keepdims=True))
                        offsets.append(jnp.sum(jnp.where(lane1 == h, offset, 0.0), 1, keepdims=True))
                    shift = jnp.where(lane1 < head_dim, offsets[0], offsets[1])
                    entering = sbuf[:, cols].astype(F32) + jnp.exp(shift) * in_ref[q, s].astype(F32)
                    carried = dot(c_part, entering.astype(BF16))
                    y = jnp.where(left, outs[0], outs[1]) + jnp.where(left, ups[0], ups[1]) * carried
                    y = y + jnp.where(lane1 < head_dim, skips[0], skips[1]) * v.astype(F32)
                    y = y * silu(gate_ref[at, cols].astype(F32))
                    g[at, cols] = y
                    acc[at, :] += y * y
                    return 0

                lax.fori_loop(0, heads // 2, pair, 0)
                return 0

            lax.fori_loop(0, per_block, one_chunk, 0)

    scale_f = lax.rsqrt(jnp.sum(accf[...], 1, keepdims=True) * (1.0 / inner) + 1e-05)
    scale_b = lax.rsqrt(jnp.sum(accb[...], 1, keepdims=True) * (1.0 / inner) + 1e-05)
    order = shuffle(True)
    for j in range(inner // TILE):
        lanes = slice(j * TILE, (j + 1) * TILE)
        value = (gf[:, lanes] * scale_f + gb[:, lanes] * scale_b) * gain_ref[:, lanes]
        value = value.astype(BF16)
        for k in range(per_block):
            at = slice(k * CHUNK, (k + 1) * CHUNK)
            normed[at, lanes] = dot(order, value[at]).astype(BF16)
    out_ref[...] = (x_ref[...].astype(F32) + dot(normed[...], w_ref[...])).astype(BF16)


def local(hidden, in_weight, conv_weight, conv_bias, step_bias, decay_rate, skip_gain, norm_gain, out_weight):
    length, width = hidden.shape
    heads = step_bias.shape[0]
    inner = out_weight.shape[0]
    head_dim = inner // heads
    conv_width = conv_weight.shape[1]
    state = (conv_width - inner) // 2
    chunks = length // CHUNK
    tiles = inner // TILE
    count = lax.axis_size("ctx")
    groups = -(-chunks * heads // 128)
    ring = range(count)
    prev = lax.ppermute(hidden[length - HALO :], "ctx", [(i, i + 1) for i in ring if i + 1 < count])
    follow = lax.ppermute(hidden[:HALO], "ctx", [(i + 1, i) for i in ring if i + 1 < count])
    sizes = (heads, head_dim, state, inner)

    def whole(shape, **kw):
        return pl.BlockSpec(shape, lambda j: (0,) * len(shape), **kw)

    def value_tile(j):
        return jnp.clip(j - 1, 0, tiles - 1)

    def conv_tile(j):
        return jnp.where(j == 0, tiles, value_tile(j))

    def weight_tile(j):
        return jnp.where(j == 0, 2 * tiles, jnp.where(j <= tiles, tiles - 1 + j, j - tiles - 1))

    def shape(dims, dtype):
        return jax.ShapeDtypeStruct(dims, dtype)

    row2 = lambda a: a.reshape(1, -1)
    once = dict(pipeline_mode=pl.Buffered(1))
    outs = pl.pallas_call(
        functools.partial(front_kernel, *sizes),
        name="front",
        grid=(1 + 2 * tiles,),
        in_specs=[
            whole((length, width), **once),
            whole((HALO, width)),
            whole((HALO, width)),
            pl.BlockSpec((TILE, width), lambda j: (weight_tile(j), 0)),
            pl.BlockSpec((heads, width), lambda j: ((inner + conv_width) // heads, 0), **once),
            pl.BlockSpec((4, TILE), lambda j: (0, conv_tile(j))),
            pl.BlockSpec((1, TILE), lambda j: (0, conv_tile(j))),
            whole((1, heads)),
            whole((1, heads)),
            whole((1, heads)),
        ],
        out_specs=[
            pl.BlockSpec((length, TILE), lambda j: (0, jnp.maximum(j - tiles - 1, 0))),
            pl.BlockSpec((length, TILE), lambda j: (0, conv_tile(j))),
            pl.BlockSpec((length, TILE), lambda j: (0, conv_tile(j))),
            pl.BlockSpec((length, TILE), lambda j: (0, value_tile(j))),
            pl.BlockSpec((length, TILE), lambda j: (0, value_tile(j))),
            pl.BlockSpec((chunks, state, TILE), lambda j: (0, 0, value_tile(j))),
            pl.BlockSpec((chunks, state, TILE), lambda j: (0, 0, value_tile(j))),
            pl.BlockSpec((TILE // 128, 2, state + 16, 128), lambda j: (value_tile(j), 0, 0, 0)),
            whole((groups, CHUNK, 256)),
            whole((groups, CHUNK, 256)),
            whole((groups, CHUNK, 128)),
            whole((4 * groups, 128)),
            pl.BlockSpec(memory_space=pltpu.SMEM),
        ],
        out_shape=[
            shape((length, inner), BF16),
            shape((length, conv_width), BF16),
            shape((length, conv_width), BF16),
            shape((length, inner), BF16),
            shape((length, inner), BF16),
            shape((chunks, state, inner), BF16),
            shape((chunks, state, inner), BF16),
            shape((inner // 128, 2, state + 16, 128), BF16),
            shape((groups, CHUNK, 256), BF16),
            shape((groups, CHUNK, 256), BF16),
            shape((groups, CHUNK, 128), F32),
            shape((4 * groups, 128), F32),
            shape((groups,), F32),
        ],
        scratch_shapes=[
            pltpu.VMEM((length + 2 * HALO, width), BF16),
            pltpu.VMEM((chunks * (CHUNK + 48), TILE), F32),
            pltpu.VMEM((8, 128), F32),
        ]
        + [pltpu.VMEM((groups, CHUNK, 256), BF16)] * 4
        + [pltpu.VMEM((length, CHUNK + state), BF16)] * 2
        + [pltpu.VMEM((chunks * state, CHUNK), BF16)] * 2
        + [pltpu.VMEM((16, 128), BF16)]
        + [pltpu.VMEM((chunks, CHUNK + state, TILE), BF16)] * 2,
        compiler_params=pltpu.CompilerParams(vmem_limit_bytes=VMEM),
    )(
        hidden, follow, prev, in_weight.T, in_weight.T, conv_weight, row2(conv_bias), row2(step_bias), row2(decay_rate),
        row2(skip_gain),
    )
    gate, xf, xb, yf, yb, sf, sb, end, ef, eb, step, off, span = outs
    entering = pl.pallas_call(
        carry_kernel,
        name="carry",
        in_specs=[pl.BlockSpec(memory_space=pltpu.VMEM)],
        out_specs=pl.BlockSpec(memory_space=pltpu.VMEM),
        out_shape=shape((count, 2, state, 128), BF16),
        scratch_shapes=[
            pltpu.VMEM((count // 2, 2, state + 16, 128), BF16),
            pltpu.VMEM((count // 2, 2, state + 16, 128), BF16),
            pltpu.VMEM((count // 2, 2, state + 16, 128), BF16),
            pltpu.VMEM((count // 2, 2, state, 128), BF16),
            pltpu.VMEM((count // 2, 2, state, 128), BF16),
            pltpu.VMEM((count // 2, 2, state, 128), BF16),
        ]
        + [pltpu.SemaphoreType.DMA((count // 2,))] * 4
        + [pltpu.SemaphoreType.DMA((2,))] * 3,
        compiler_params=pltpu.CompilerParams(collective_id=0, has_side_effects=True, vmem_limit_bytes=VMEM),
    )(end)
    anywhere = pl.BlockSpec(memory_space=pl.ANY)
    block = pl.BlockSpec((ROWS, inner), lambda j: (j, 0))
    c_block = pl.BlockSpec((ROWS, state), lambda j: (j, inner // state + 1))
    e_block = pl.BlockSpec((1, CHUNK, 256), lambda j: (j * (ROWS // CHUNK) // (128 // heads), 0, 0))
    return pl.pallas_call(
        functools.partial(back_kernel, *sizes),
        name="back",
        grid=(length // ROWS,),
        in_specs=[
            pl.BlockSpec(memory_space=pltpu.SMEM),
            block, block, block, c_block, c_block, e_block, e_block,
            whole((count, 2, state, 128), **once),
            pl.BlockSpec((ROWS, width), lambda j: (j, 0)),
            whole((inner, width), **once),
            whole((1, inner)),
            whole((1, heads)),
            whole((1, heads)),
            whole((4 * groups, 128)),
        ]
        + [anywhere] * 5,
        out_specs=pl.BlockSpec((ROWS, width), lambda j: (j, 0)),
        out_shape=shape((length, width), BF16),
        scratch_shapes=[
            pltpu.VMEM((ROWS, inner), F32),
            pltpu.VMEM((ROWS, inner), F32),
            pltpu.VMEM((ROWS, 128), F32),
            pltpu.VMEM((ROWS, 128), F32),
            pltpu.VMEM((ROWS, inner), BF16),
            pltpu.VMEM((8, 128), F32),
            pltpu.VMEM((CHUNK, conv_width), BF16),
            pltpu.VMEM((state, inner), BF16),
            pltpu.VMEM((CHUNK, 128), F32),
            pltpu.SemaphoreType.DMA((3,)),
        ],
        compiler_params=pltpu.CompilerParams(vmem_limit_bytes=VMEM),
    )(
        span, yf, yb, gate, xf, xb, ef, eb, entering, hidden, out_weight, row2(norm_gain), row2(decay_rate),
        row2(skip_gain), off, xf, xb, sf, sb, step,
    )


def solution(mesh):
    return jax.shard_map(
        local,
        mesh=mesh,
        in_specs=(P(("dp", "ctx"), None), P(), P(), P(), P(), P(), P(), P(), P()),
        out_specs=P(("dp", "ctx"), None),
        check_vma=False,
    )
```

time: 124 us -> 90.1 us (0.73)
  Pallas kernels: 99 us -> 78.2 us
  local copies, waits for them, and re-layouts: 17.7 us -> 2.64 us
  waiting for transfers between devices: 0.01 us -> 1.82 us
    unnamed x23 -> x4, local copies, waits for them, and re-layouts: 16.3 us -> 0.6 us
    pallas_call x1, Pallas kernels: 46.9 us -> 34.1 us  [local(): pl.pallas_call(functools.partial(front_kernel, *sizes), name='front', gri...]
    pallas_call x1, Pallas kernels: 39 us -> 29.1 us  [local(): pl.pallas_call(carry_kernel, name='carry', in_specs=[pl.BlockSpec(memory_...]
    pallas_call x1, Pallas kernels: 13.1 us -> 15.1 us  [local(): pl.pallas_call(functools.partial(back_kernel, *sizes), name='back', grid=...]
    ppermute x1, waiting for transfers between devices: 0.01 us -> 1.82 us  [local(): lax.ppermute(hidden[:HALO], 'ctx', [(i + 1, i) for i in ring if i + 1 < c...]
  transfers between devices with their start and end apart: 2 -> 2, of which waited for: 0 -> 1; matrix products, arithmetic and copies ran while one was open for 10% -> 1% of each run, Pallas kernels for 0% -> 0%
where the time goes in v2:
time: 90.1 us; the launch traced here: 89.6 us
  Pallas kernels  78.2 us (87%)
  starting transfers between devices  6.83 us (8%)
  local copies, waits for them, and re-layouts  2.64 us (3%)
  waiting for transfers between devices  1.82 us (2%)
    pallas_call x1, Pallas kernels, local(): pl.pallas_call(functools.partial(front_kernel, *sizes), name='front', gri...  34.1 us
    pallas_call x1, Pallas kernels, local(): pl.pallas_call(carry_kernel, name='carry', in_specs=[pl.BlockSpec(memory_...  29.1 us
    pallas_call x1, Pallas kernels, local(): pl.pallas_call(functools.partial(back_kernel, *sizes), name='back', grid=...  15.1 us
    ppermute x1, starting transfers between devices, local(): lax.ppermute(hidden[length - HALO:], 'ctx', [(i, i + 1) for i in ring if...  4.91 us
    ppermute x1, starting transfers between devices, local(): lax.ppermute(hidden[:HALO], 'ctx', [(i + 1, i) for i in ring if i + 1 < c...  1.92 us
    ppermute x1, waiting for transfers between devices, local(): lax.ppermute(hidden[:HALO], 'ctx', [(i + 1, i) for i in ring if i + 1 < c...  1.82 us
  transfers between devices with their start and end apart: 2, of which 1 were waited for; matrix products, arithmetic and copies ran while one was open for 1% of the time, Pallas kernels for 0%

profile of v2, /device:TPU:1, one launch (start us, length us, event | category | flops | bytes accessed | tf_op | source)
XLA Modules:
  0.0 89.6 jit_solution(7527879769364752715)
XLA Ops:
  0.0 0.7 fusion
  0.7 4.9 %collective-permute-start.1 = (bf16[8,1024]{1,0:T(8,128)(2,1)S(1)}, bf16[8,1024]{1,0:T(8,128)(2,1)S(1)}, u32[]{:S(2)}, u32[]{:S(2)}) collective-permute-start(bf16[8,1024]{1,0:T(8,128)(2,1)S(1)} %get-tuple-element.31), channel_id=1, source_target_pairs={{0,8},{8,16},{16,24},{24,32},{32,40},{40,48},{48,56},{56,64},{64,7... | collective-permute-start | bytes 49160 | tf_op jit(solution)/shard_map/ppermute | solution.py:490
  5.7 1.9 %collective-permute-start = (bf16[8,1024]{1,0:T(8,128)(2,1)S(1)}, bf16[8,1024]{1,0:T(8,128)(2,1)S(1)}, u32[]{:S(2)}, u32[]{:S(2)}) collective-permute-start(bf16[8,1024]{1,0:T(8,128)(2,1)S(1)} %get-tuple-element.32), channel_id=1, source_target_pairs={{8,0},{16,8},{24,16},{32,24},{40,32},{48,40},{56,48},{64,56},{72,6... | collective-permute-start | bytes 49160 | tf_op jit(solution)/shard_map/ppermute | solution.py:491
  7.6 1.3 %reshape.17.cb_ref = f32[1,2304]{1,0:T(1,128)} reshape(f32[2304]{0:T(1024)} %param.12) | data formatting | bytes 18432 | tf_op jit(solution)/shard_map/reshape | solution.py:509
  8.9 0.0 collective-permute-done.1.prev_ref
  8.9 0.0 copy-start
  8.9 1.8 %collective-permute-done.next_ref = bf16[8,1024]{1,0:T(8,128)(2,1)S(1)} collective-permute-done((bf16[8,1024]{1,0:T(8,128)(2,1)S(1)}, bf16[8,1024]{1,0:T(8,128)(2,1)S(1)}, u32[]{:S(2)}, u32[]{:S(2)}) %collective-permute-start) | collective-permute-done | bytes 16416 | tf_op jit(solution)/shard_map/ppermute | solution.py:491
  10.7 0.0 copy-start.1
  10.7 0.0 copy-done
  10.7 0.6 copy-done.1
  11.3 34.1 %front.1 = (bf16[768,2048]{1,0:T(8,128)(2,1)}, bf16[768,2304]{1,0:T(8,128)(2,1)}, bf16[768,2304]{1,0:T(8,128)(2,1)}, bf16[768,2048]{1,0:T(8,128)(2,1)}, bf16[768...) custom-call(bf16[768,1024]{1,0:T(8,128)(2,1)} %x_ref.3, ...), custom_call_target="tpu_custom_call" | custom-call | tf_op jit(solution)/shard_map/front/pallas_call | solution.py:511
  45.5 29.1 %carry.1.in_ref = bf16[16,2,128,128]{3,2,1,0:T(8,128)(2,1)} custom-call(bf16[16,2,144,128]{3,2,1,0:T(8,128)(2,1)} %get-tuple-element.26.end_ref), custom_call_target="tpu_custom_call" | custom-call | tf_op jit(solution)/shard_map/carry/pallas_call | solution.py:573
  74.5 15.1 %back.1 = bf16[768,1024]{1,0:T(8,128)(2,1)} custom-call(f32[2]{0:T(128)} %get-tuple-element.18.span_ref, bf16[768,2048]{1,0:T(8,128)(2,1)} %get-tuple-element.19.yf_ref, bf16[768,2048]{1,0:T(8,128)(2,1)} %get-tuple-element.20.yb_ref, bf16[768,2048]{1,0:T(8,128)(2,1)} %get-tuple-element.21.gate_ref, bf16[768,2304]{1,0:T(8,128)(2,1)} %get-tuple-element.22.cf_ref.xf_any, ...), custom_call_target="tpu_custom_call" | custom-call | tf_op jit(solution)/shard_map/back/pallas_call | solution.py:595
Async XLA Ops:
  0.7 8.2 %collective-permute-start.1 = (bf16[8,1024]{1,0:T(8,128)(2,1)S(1)}, bf16[8,1024]{1,0:T(8,128)(2,1)S(1)}, u32[]{:S(2)}, u32[]{:S(2)}) collective-permute-start(bf16[8,1024]{1,0:T(8,128)(2,1)S(1)} %get-tuple-element.31), channel_id=1, source_target_pairs={{0,8},{8,16},{16,24},{24,32},{32,40},{40,48},{48,56},{56,64},{64,7... | collective-permute-start | bytes 49160 | tf_op jit(solution)/shard_map/ppermute | solution.py:490
  5.7 5.1 %collective-permute-start = (bf16[8,1024]{1,0:T(8,128)(2,1)S(1)}, bf16[8,1024]{1,0:T(8,128)(2,1)S(1)}, u32[]{:S(2)}, u32[]{:S(2)}) collective-permute-start(bf16[8,1024]{1,0:T(8,128)(2,1)S(1)} %get-tuple-element.32), channel_id=1, source_target_pairs={{8,0},{16,8},{24,16},{32,24},{40,32},{48,40},{56,48},{64,56},{72,6... | collective-permute-start | bytes 49160 | tf_op jit(solution)/shard_map/ppermute | solution.py:491
  8.9 1.8 %copy-start = (bf16[8,1024]{1,0:T(8,128)(2,1)}, bf16[8,1024]{1,0:T(8,128)(2,1)S(1)}, u32[]{:S(2)}) copy-start(bf16[8,1024]{1,0:T(8,128)(2,1)S(1)} %collective-permute-done.1.prev_ref) | copy-start | bytes 49156
  10.7 0.6 copy-start.1

commit v3 on v2

--- a/solution.py
+++ b/solution.py
@@ -72,9 +72,11 @@
 
 
 def front_kernel(
-    heads, head_dim, state, inner, x_ref, next_ref, prev_ref, w_ref, wdt_ref, cw_ref, cb_ref, bias_ref, decay_ref, skip_ref,
-    gate_ref, xf_ref, xb_ref, yf_ref, yb_ref, sf_ref, sb_ref, end_ref, ef_ref, eb_ref, step_ref, off_ref, span_ref,
-    hx, xs, par, wf, wb, of, ob, gcf, gcb, btf, btb, small, rhsf, rhsb,
+    heads, head_dim, state, inner, x_ref, w_ref, wdt_ref, cw_ref, cb_ref, bias_ref, decay_ref, skip_ref,
+    gate_ref, xf_ref, xb_ref, yf_ref, yb_ref, sf_ref, sb_ref, in_ref, ef_ref, eb_ref, step_ref, off_ref, span_ref,
+    hx, xs, par, wf, wb, of, ob, gcf, gcb, btf, btb, small, rhs, kept_x, ends,
+    follow, before_me, paired, chip, arrived, answers, entering, other, landed,
+    halo_out, halo_in, pair_out, pair_in, first_out, first_in, second_out, second_in, back_out, back_in, own_sem,
 ):
     length = x_ref.shape[0]
     chunks = length // CHUNK
@@ -84,6 +86,130 @@
     edge = 24
     span = CHUNK + 2 * edge
     j = pl.program_id(0)
+    count = lax.axis_size("ctx")
+    me = lax.axis_index("ctx")
+    core, mine = lax.rem(me, 2), lax.div(me, 2)
+    partner = me + 1 - 2 * core
+    low = core == 0
+    peers = count // 2
+    chips = [lax.rem(mine + d, peers) for d in range(1, peers)]
+    half_tiles = tiles // 2
+    per_tile = TILE // 128
+
+    def send(src, dst, out_sem, in_sem, peer):
+        return pltpu.make_async_remote_copy(
+            src_ref=src, dst_ref=dst, send_sem=out_sem, recv_sem=in_sem, device_id={"ctx": peer}, device_id_type=MESH
+        )
+
+    def halos():
+        edge_rows = follow.shape[0]
+        return [
+            send(x_ref.at[:edge_rows], follow, halo_out.at[0], halo_in.at[0], lax.rem(me + count - 1, count)),
+            send(
+                x_ref.at[length - edge_rows :], before_me, halo_out.at[1], halo_in.at[1], lax.rem(me + 1, count)
+            ),
+        ]
+
+    def pair_copy(t):
+        at = pl.ds(t * per_tile, per_tile)
+        slot = lax.rem(t, half_tiles)
+        return send(
+            ends.at[at], paired.at[pl.ds(slot * per_tile, per_tile)], pair_out.at[slot], pair_in.at[slot], partner
+        )
+
+    def total(ref, k):
+        rows = ref[k, 0, state : state + 16, :].astype(F32)
+        return rows[0:1] + rows[1:2] + rows[2:3]
+
+    def first_copy(k):
+        return send(chip.at[k], arrived.at[mine], first_out.at[k], first_in.at[mine], 2 * k + core)
+
+    def combine(t):
+        slot = lax.rem(t, half_tiles)
+        pair_copy(t).wait_recv()
+        for half in range(per_tile):
+            k = slot * per_tile + half
+            at = core * peers + k
+            t_own, t_part = total(ends, at), total(paired, k)
+            f_own, f_part = jnp.exp(t_own), jnp.exp(t_part)
+            one = jnp.ones_like(f_own)
+            own0, part0 = ends[at, 0, :state, :].astype(F32), paired[k, 0, :state, :].astype(F32)
+            own1, part1 = ends[at, 1, :state, :].astype(F32), paired[k, 1, :state, :].astype(F32)
+            chip[k, 0, :state, :] = (
+                own0 * jnp.where(low, f_part, one) + part0 * jnp.where(low, one, f_own)
+            ).astype(BF16)
+            chip[k, 1, :state, :] = (
+                own1 * jnp.where(low, one, f_part) + part1 * jnp.where(low, f_own, one)
+            ).astype(BF16)
+            extra = jnp.concatenate(three_terms(t_own + t_part) + [jnp.zeros((13, 128), F32)], 0).astype(BF16)
+            chip[k, 0, state:, :] = extra
+            chip[k, 1, state:, :] = extra
+
+            @pl.when(k != mine)
+            def _():
+                first_copy(k).start()
+
+            @pl.when(k == mine)
+            def _():
+                pltpu.make_async_copy(chip.at[k], arrived.at[k], own_sem.at[0]).start()
+
+    def second_copy(k):
+        return send(answers.at[k], entering.at[mine], second_out.at[k], second_in.at[mine], 2 * k + core)
+
+    def scan():
+        pltpu.make_async_copy(chip.at[mine], arrived.at[mine], own_sem.at[0]).wait()
+        for k in chips:
+            send(chip.at[k], arrived.at[k], first_out.at[k], first_in.at[k], 2 * k + core).wait_recv()
+        for strand, order in ((0, list(range(peers))), (1, list(reversed(range(peers))))):
+            running = jnp.zeros((state, 128), F32)
+            for k in order:
+                answers[k, strand] = running.astype(BF16)
+                if k != order[-1]:
+                    running = jnp.exp(total(arrived, k)) * running + arrived[k, strand, :state, :].astype(F32)
+        for k in chips:
+            second_copy(k).start()
+        pltpu.make_async_copy(answers.at[mine], entering.at[mine], own_sem.at[1]).start()
+
+    def back_copy():
+        return send(other, landed, back_out.at[0], back_in.at[0], partner)
+
+    def enter():
+        pltpu.make_async_copy(answers.at[mine], entering.at[mine], own_sem.at[1]).wait()
+        for k in chips:
+            send(answers.at[k], entering.at[k], second_out.at[k], second_in.at[k], 2 * k + core).wait_recv()
+
+        def one_pair(k, _):
+            at = core * peers + k
+            f_own, f_part = jnp.exp(total(ends, at)), jnp.exp(total(paired, k))
+            chip_f, chip_b = entering[k, 0].astype(F32), entering[k, 1].astype(F32)
+            own_late_f = f_part * chip_f + paired[k, 0, :state, :].astype(F32)
+            part_late_f = f_own * chip_f + ends[at, 0, :state, :].astype(F32)
+            own_late_b = f_part * chip_b + paired[k, 1, :state, :].astype(F32)
+            part_late_b = f_own * chip_b + ends[at, 1, :state, :].astype(F32)
+            in_ref[at, 0] = jnp.where(low, chip_f, own_late_f).astype(BF16)
+            other[k, 0] = jnp.where(low, part_late_f, chip_f).astype(BF16)
+            in_ref[at, 1] = jnp.where(low, own_late_b, chip_b).astype(BF16)
+            other[k, 1] = jnp.where(low, chip_b, part_late_b).astype(BF16)
+            return 0
+
+        lax.fori_loop(0, peers, one_pair, 0)
+        back_copy().start()
+
+    def finish():
+        back_copy().wait()
+
+        def one_pair(k, _):
+            in_ref[(1 - core) * peers + k] = landed[k]
+            return 0
+
+        lax.fori_loop(0, peers, one_pair, 0)
+        for copy in halos():
+            copy.wait_send()
+        for slot in range(half_tiles):
+            pair_copy((1 - core) * half_tiles + slot).wait_send()
+        for k in chips:
+            first_copy(k).wait_send()
+            second_copy(k).wait_send()
 
     def project():
         out = dot_nt(hx[...], w_ref[...])
@@ -121,19 +247,22 @@
 
     @pl.when(j == 0)
     def _():
+        barrier = pltpu.get_barrier_semaphore()
+        beside = lax.rem(me + count - 1 + 2 * core, count)
+        for peer in [partner, beside] + [2 * k + core for k in chips]:
+            pl.semaphore_signal(barrier, inc=1, device_id={"ctx": peer}, device_id_type=MESH)
+        pl.semaphore_wait(barrier, peers + 1)
+        for copy in halos():
+            copy.start()
         order = shuffle(False)
         for c in range(chunks):
             rows = slice(c * CHUNK, (c + 1) * CHUNK)
             hx[rows] = dot(order, x_ref[rows]).astype(BF16)
-        hx[length:] = jnp.concatenate(
-            [next_ref[...].astype(F32), prev_ref[...].astype(F32)], 0
-        ).astype(BF16)
         par[...] = jnp.zeros_like(par)
         for q in range(packs):
             par[0:1, q * heads : (q + 1) * heads] = bias_ref[...]
             par[1:2, q * heads : (q + 1) * heads] = decay_ref[...]
         par[2:3, :heads] = skip_ref[...]
-        project()
         lower = jnp.where(triangle(True), 1.0, 0.0)
         upper = jnp.where(triangle(False), 1.0, 0.0)
         lane1 = iota((1, 128), 1)
@@ -200,6 +329,18 @@
         lines += three_terms(slab) + three_terms(par[2:3, :])
         lines.append(jnp.zeros((16 - len(lines), 128), F32))
         small[...] = jnp.concatenate(lines, 0).astype(BF16)
+        for copy in halos():
+            copy.wait_recv()
+        first_row = jnp.where(me == count - 1, 0.0, 1.0)
+        last_row = jnp.where(me == 0, 0.0, 1.0)
+        hx[length:] = jnp.concatenate(
+            [
+                follow[...].astype(F32)[:HALO] * first_row,
+                before_me[...].astype(F32)[before_me.shape[0] - HALO :] * last_row,
+            ],
+            0,
+        ).astype(BF16)
+        project()
         for c in range(chunks):
             rows = slice(c * CHUNK, (c + 1) * CHUNK)
             forward, backward = convolved(c)
@@ -214,10 +355,24 @@
                 gc[rows, CHUNK:] = c_part
                 bt[rows, :] = value[:, :state].T.astype(BF16)
 
+    first = lax.rem(j - 1, tiles) * (TILE // head_dim)
+
+    @pl.when((j >= 2) & (j <= tiles + 1) & (lax.div(j - 2, half_tiles) == core))
+    def _():
+        combine(j - 2)
+
+    @pl.when(j == tiles + 1 + core * half_tiles)
+    def _():
+        scan()
+
+    @pl.when((j == tiles + 1 + half_tiles) & low)
+    def _():
+        enter()
+
     @pl.when((j > 0) & (j <= tiles))
     def _():
+        t = j - 1
         project()
-        first = (j - 1) * (TILE // head_dim)
         spreads = [spread_matrix(first + q * heads, head_dim, 256) for q in range(packs)]
         lines = [dot(small[...], spread[:128]) for spread in spreads]
 
@@ -226,137 +381,57 @@
             return rows[0:1] + rows[1:2] + rows[2:3]
 
         fade = [line(c % packs, c // packs) for c in range(chunks)]
-        slab, skip = line(0, groups), line(0, groups + 1)
+        slab = line(0, groups)
         for c in range(chunks):
             rows = slice(c * CHUNK, (c + 1) * CHUNK)
             g, spread = c // packs, spreads[c % packs]
-            forward, backward = convolved(c)
-            xf_ref[rows, :] = forward.astype(BF16)
-            xb_ref[rows, :] = backward.astype(BF16)
-            rhsf[c, :CHUNK] = (forward * dot(wf[g], spread)).astype(BF16)
-            rhsb[c, :CHUNK] = (backward * dot(wb[g], spread)).astype(BF16)
-        ends = []
-        for order, s_ref, bt, rhs in (
-            (range(chunks), sf_ref, btf, rhsf),
-            (reversed(range(chunks)), sb_ref, btb, rhsb),
+            for strand, (value, x_out, w) in enumerate(zip(convolved(c), (xf_ref, xb_ref), (wf, wb))):
+                rounded = value.astype(BF16)
+                x_out[rows, :] = rounded
+                kept_x[strand, t, rows] = rounded
+                rhs[strand, t, c, :CHUNK] = (value * dot(w[g], spread)).astype(BF16)
+        extra = jnp.concatenate(three_terms(slab) + [jnp.zeros((13, TILE), F32)], 0).astype(BF16)
+        for strand, (order, s_ref, bt) in enumerate(
+            ((range(chunks), sf_ref, btf), (reversed(range(chunks)), sb_ref, btb))
         ):
             running = jnp.zeros((state, TILE), F32)
             for c in order:
                 rows = slice(c * CHUNK, (c + 1) * CHUNK)
                 decayed = running * fade[c]
                 s_ref[c] = running.astype(BF16)
-                rhs[c, CHUNK:] = decayed.astype(BF16)
-                running = decayed + dot(bt[rows, :], rhs[c, :CHUNK])
-            ends.append(running)
-        extra = jnp.concatenate(three_terms(slab) + [jnp.zeros((13, TILE), F32)], 0).astype(BF16)
-        for strand in range(2):
-            for half in range(TILE // 128):
+                rhs[strand, t, c, CHUNK:] = decayed.astype(BF16)
+                running = decayed + dot(bt[rows, :], rhs[strand, t, c, :CHUNK])
+            for half in range(per_tile):
                 lanes = slice(half * 128, (half + 1) * 128)
-                end_ref[half, strand, :state, :] = ends[strand][:, lanes].astype(BF16)
-                end_ref[half, strand, state:, :] = extra[:, lanes]
+                ends[t * per_tile + half, strand, :state, :] = running[:, lanes].astype(BF16)
+                ends[t * per_tile + half, strand, state:, :] = extra[:, lanes]
+
+    @pl.when((j > 0) & (j <= tiles) & (lax.div(j - 1, half_tiles) != core))
+    def _():
+        pair_copy(j - 1).start()
+
+    @pl.when(j > tiles)
+    def _():
+        t = j - 1 - tiles
+        gate_ref[...] = dot_nt(hx[:length], w_ref[...]).astype(BF16)
+        spreads = [spread_matrix(first + q * heads, head_dim, 256) for q in range(packs)]
+        rows3 = dot(small[...], spreads[0][:128])[3 * groups + 3 : 3 * groups + 6]
+        skip = rows3[0:1] + rows3[1:2] + rows3[2:3]
         for c in range(chunks):
             rows = slice(c * CHUNK, (c + 1) * CHUNK)
             g, spread = c // packs, spreads[c % packs]
-            for y_ref, x_out, gc, rhs, o in (
-                (yf_ref, xf_ref, gcf, rhsf, of),
-                (yb_ref, xb_ref, gcb, rhsb, ob),
-            ):
-                mixed = dot(gc[rows, :], rhs[c])
-                y_ref[rows, :] = (mixed * dot(o[g], spread) + skip * x_out[rows, :].astype(F32)).astype(BF16)
-
-    @pl.when(j > tiles)
-    def _():
-        gate_ref[...] = dot_nt(hx[:length], w_ref[...]).astype(BF16)
-
-
-def carry_kernel(
-    end_ref, in_ref, paired, chip, arrived, answers, entering, other, out_sem, in_sem, out_sem2, in_sem2, pair_out, pair_in,
-    own_sem,
-):
-    pairs = end_ref.shape[0]
-    state = in_ref.shape[2]
-    count = pairs // 2
-    me = lax.axis_index("ctx")
-    core, mine = lax.rem(me, 2), lax.div(me, 2)
-    partner = me + 1 - 2 * core
-    barrier = pltpu.get_barrier_semaphore()
-    chips = [lax.rem(mine + d, count) for d in range(1, count)]
-    for peer in [partner] + [2 * k + core for k in chips]:
-        pl.semaphore_signal(barrier, inc=1, device_id={"ctx": peer}, device_id_type=MESH)
-    pl.semaphore_wait(barrier, count)
-
-    def send(src, dst, sems, sem_to, peer):
-        return pltpu.make_async_remote_copy(
-            src_ref=src, dst_ref=dst, send_sem=sems, recv_sem=sem_to, device_id={"ctx": peer}, device_id_type=MESH
-        )
-
-    swap = send(
-        end_ref.at[pl.ds((1 - core) * count, count)], paired, pair_out.at[0], pair_in.at[0], partner
-    )
-    swap.start()
-    swap.wait()
-
-    def total(ref, k):
-        rows = ref[k, 0, state : state + 16, :].astype(F32)
-        return rows[0:1] + rows[1:2] + rows[2:3]
-
-    low = core == 0
-
-    for k in range(count):
-        at = core * count + k
-        t_own, t_part = total(end_ref, at), total(paired, k)
-        f_own, f_part = jnp.exp(t_own), jnp.exp(t_part)
-        one = jnp.ones_like(f_own)
-        own0, part0 = end_ref[at, 0, :state, :].astype(F32), paired[k, 0, :state, :].astype(F32)
-        own1, part1 = end_ref[at, 1, :state, :].astype(F32), paired[k, 1, :state, :].astype(F32)
-        ahead, behind = jnp.where(low, f_part, one), jnp.where(low, one, f_own)
-        chip[k, 0, :state, :] = (own0 * ahead + part0 * behind).astype(BF16)
-        ahead, behind = jnp.where(low, one, f_part), jnp.where(low, f_own, one)
-        chip[k, 1, :state, :] = (own1 * ahead + part1 * behind).astype(BF16)
-        extra = jnp.concatenate(three_terms(t_own + t_part) + [jnp.zeros((13, 128), F32)], 0).astype(BF16)
-        chip[k, 0, state:, :] = extra
-        chip[k, 1, state:, :] = extra
-    first = [send(chip.at[k], arrived.at[mine], out_sem.at[k], in_sem.at[mine], 2 * k + core) for k in chips]
-    for copy in first:
-        copy.start()
-    own = pltpu.make_async_copy(chip.at[mine], arrived.at[mine], own_sem.at[0])
-    own.start()
-    own.wait()
-    for k in chips:
-        send(chip.at[k], arrived.at[k], out_sem.at[k], in_sem.at[k], 2 * k + core).wait_recv()
-    for strand, order in ((0, list(range(count))), (1, list(reversed(range(count))))):
-        running = jnp.zeros((state, 128), F32)
-        for k in order:
-            answers[k, strand] = running.astype(BF16)
-            if k != order[-1]:
-                running = jnp.exp(total(arrived, k)) * running + arrived[k, strand, :state, :].astype(F32)
-    second = [send(answers.at[k], entering.at[mine], out_sem2.at[k], in_sem2.at[mine], 2 * k + core) for k in chips]
-    for copy in second:
-        copy.start()
-    own = pltpu.make_async_copy(answers.at[mine], entering.at[mine], own_sem.at[1])
-    own.start()
-    own.wait()
-    for k in chips:
-        send(answers.at[k], entering.at[k], out_sem2.at[k], in_sem2.at[k], 2 * k + core).wait_recv()
-    for k in range(count):
-        at = core * count + k
-        f_own, f_part = jnp.exp(total(end_ref, at)), jnp.exp(total(paired, k))
-        chip_f, chip_b = entering[k, 0].astype(F32), entering[k, 1].astype(F32)
-        own_late_f = f_part * chip_f + paired[k, 0, :state, :].astype(F32)
-        part_late_f = f_own * chip_f + end_ref[at, 0, :state, :].astype(F32)
-        own_late_b = f_part * chip_b + paired[k, 1, :state, :].astype(F32)
-        part_late_b = f_own * chip_b + end_ref[at, 1, :state, :].astype(F32)
-        in_ref[at, 0] = jnp.where(low, chip_f, own_late_f).astype(BF16)
-        other[k, 0] = jnp.where(low, part_late_f, chip_f).astype(BF16)
-        in_ref[at, 1] = jnp.where(low, own_late_b, chip_b).astype(BF16)
-        other[k, 1] = jnp.where(low, chip_b, part_late_b).astype(BF16)
-    swap_back = send(other, in_ref.at[pl.ds(core * count, count)], pair_out.at[1], pair_in.at[1], partner)
-    swap_back.start()
-    swap_back.wait()
-    for copy in first:
-        copy.wait_send()
-    for copy in second:
-        copy.wait_send()
+            for strand, (y_ref, gc, o) in enumerate(((yf_ref, gcf, of), (yb_ref, gcb, ob))):
+                mixed = dot(gc[rows, :], rhs[strand, t, c])
+                y = mixed * dot(o[g], spread) + skip * kept_x[strand, t, rows].astype(F32)
+                y_ref[rows, :] = y.astype(BF16)
+
+    @pl.when(j == 2 * tiles)
+    def _():
+        @pl.when(jnp.logical_not(low))
+        def _():
+            enter()
+
+        finish()
 
 
 def back_kernel(
@@ -486,9 +561,6 @@
     tiles = inner // TILE
     count = lax.axis_size("ctx")
     groups = -(-chunks * heads // 128)
-    ring = range(count)
-    prev = lax.ppermute(hidden[length - HALO :], "ctx", [(i, i + 1) for i in ring if i + 1 < count])
-    follow = lax.ppermute(hidden[:HALO], "ctx", [(i + 1, i) for i in ring if i + 1 < count])
     sizes = (heads, head_dim, state, inner)
 
     def whole(shape, **kw):
@@ -514,8 +586,6 @@
         grid=(1 + 2 * tiles,),
         in_specs=[
             whole((length, width), **once),
-            whole((HALO, width)),
-            whole((HALO, width)),
             pl.BlockSpec((TILE, width), lambda j: (weight_tile(j), 0)),
             pl.BlockSpec((heads, width), lambda j: ((inner + conv_width) // heads, 0), **once),
             pl.BlockSpec((4, TILE), lambda j: (0, conv_tile(j))),
@@ -528,11 +598,11 @@
             pl.BlockSpec((length, TILE), lambda j: (0, jnp.maximum(j - tiles - 1, 0))),
             pl.BlockSpec((length, TILE), lambda j: (0, conv_tile(j))),
             pl.BlockSpec((length, TILE), lambda j: (0, conv_tile(j))),
-            pl.BlockSpec((length, TILE), lambda j: (0, value_tile(j))),
-            pl.BlockSpec((length, TILE), lambda j: (0, value_tile(j))),
+            pl.BlockSpec((length, TILE), lambda j: (0, jnp.maximum(j - tiles - 1, 0))),
+            pl.BlockSpec((length, TILE), lambda j: (0, jnp.maximum(j - tiles - 1, 0))),
             pl.BlockSpec((chunks, state, TILE), lambda j: (0, 0, value_tile(j))),
             pl.BlockSpec((chunks, state, TILE), lambda j: (0, 0, value_tile(j))),
-            pl.BlockSpec((TILE // 128, 2, state + 16, 128), lambda j: (value_tile(j), 0, 0, 0)),
+            whole((count, 2, state, 128)),
             whole((groups, CHUNK, 256)),
             whole((groups, CHUNK, 256)),
             whole((groups, CHUNK, 128)),
@@ -547,7 +617,7 @@
             shape((length, inner), BF16),
             shape((chunks, state, inner), BF16),
             shape((chunks, state, inner), BF16),
-            shape((inner // 128, 2, state + 16, 128), BF16),
+            shape((count, 2, state, 128), BF16),
             shape((groups, CHUNK, 256), BF16),
             shape((groups, CHUNK, 256), BF16),
             shape((groups, CHUNK, 128), F32),
@@ -563,31 +633,24 @@
         + [pltpu.VMEM((length, CHUNK + state), BF16)] * 2
         + [pltpu.VMEM((chunks * state, CHUNK), BF16)] * 2
         + [pltpu.VMEM((16, 128), BF16)]
-        + [pltpu.VMEM((chunks, CHUNK + state, TILE), BF16)] * 2,
-        compiler_params=pltpu.CompilerParams(vmem_limit_bytes=VMEM),
+        + [
+            pltpu.VMEM((2, tiles, chunks, CHUNK + state, TILE), BF16),
+            pltpu.VMEM((2, tiles, length, TILE), BF16),
+            pltpu.VMEM((count, 2, state + 16, 128), BF16),
+            pltpu.VMEM((16, width), BF16),
+            pltpu.VMEM((16, width), BF16),
+        ]
+        + [pltpu.VMEM((count // 2, 2, state + 16, 128), BF16)] * 3
+        + [pltpu.VMEM((count // 2, 2, state, 128), BF16)] * 4
+        + [pltpu.SemaphoreType.DMA((n,)) for n in (2, 2, tiles // 2, tiles // 2)]
+        + [pltpu.SemaphoreType.DMA((count // 2,))] * 4
+        + [pltpu.SemaphoreType.DMA((n,)) for n in (1, 1, 2)],
+        compiler_params=pltpu.CompilerParams(collective_id=0, has_side_effects=True, vmem_limit_bytes=VMEM),
     )(
-        hidden, follow, prev, in_weight.T, in_weight.T, conv_weight, row2(conv_bias), row2(step_bias), row2(decay_rate),
+        hidden, in_weight.T, in_weight.T, conv_weight, row2(conv_bias), row2(step_bias), row2(decay_rate),
         row2(skip_gain),
     )
-    gate, xf, xb, yf, yb, sf, sb, end, ef, eb, step, off, span = outs
-    entering = pl.pallas_call(
-        carry_kernel,
-        name="carry",
-        in_specs=[pl.BlockSpec(memory_space=pltpu.VMEM)],
-        out_specs=pl.BlockSpec(memory_space=pltpu.VMEM),
-        out_shape=shape((count, 2, state, 128), BF16),
-        scratch_shapes=[
-            pltpu.VMEM((count // 2, 2, state + 16, 128), BF16),
-            pltpu.VMEM((count // 2, 2, state + 16, 128), BF16),
-            pltpu.VMEM((count // 2, 2, state + 16, 128), BF16),
-            pltpu.VMEM((count // 2, 2, state, 128), BF16),
-            pltpu.VMEM((count // 2, 2, state, 128), BF16),
-            pltpu.VMEM((count // 2, 2, state, 128), BF16),
-        ]
-        + [pltpu.SemaphoreType.DMA((count // 2,))] * 4
-        + [pltpu.SemaphoreType.DMA((2,))] * 3,
-        compiler_params=pltpu.CompilerParams(collective_id=0, has_side_effects=True, vmem_limit_bytes=VMEM),
-    )(end)
+    gate, xf, xb, yf, yb, sf, sb, entering, ef, eb, step, off, span = outs
     anywhere = pl.BlockSpec(memory_space=pl.ANY)
     block = pl.BlockSpec((ROWS, inner), lambda j: (j, 0))
     c_block = pl.BlockSpec((ROWS, state), lambda j: (j, inner // state + 1))

time: 90.1 us -> 65.3 us (0.72)
  Pallas kernels: 78.2 us -> 63.6 us
  starting transfers between devices: 6.83 us -> 0 us
  waiting for transfers between devices: 1.82 us -> 0 us
  local copies, waits for them, and re-layouts: 2.64 us -> 1.31 us
    pallas_call x1 -> x0, Pallas kernels: 29.1 us -> none  [local(): pl.pallas_call(carry_kernel, name='carry', in_specs=[pl.BlockSpec(memory_...]
    pallas_call x1, Pallas kernels: 34.1 us -> 48.6 us  [local(): pl.pallas_call(functools.partial(front_kernel, *sizes), name='front', gri...]
    ppermute x2 -> x0, starting transfers between devices: 6.83 us -> none  [the longest x1 4.91 us: local(): lax.ppermute(hidden[length - HALO:], 'ctx', [(i, i + 1) for i in ring if...]
    ppermute x2 -> x0, waiting for transfers between devices: 1.82 us -> none  [the longest x1 1.82 us: local(): lax.ppermute(hidden[:HALO], 'ctx', [(i + 1, i) for i in ring if i + 1 < c...]
  transfers between devices with their start and end apart: 2 -> 0, of which waited for: 1 -> 0; matrix products, arithmetic and copies ran while one was open for 1% -> 0% of each run, Pallas kernels for 0% -> 0%
where the time goes in v3:
time: 65.3 us; the launch traced here: 64.9 us
  Pallas kernels  63.6 us (97%)
  local copies, waits for them, and re-layouts  1.31 us (2%)
    pallas_call x1, Pallas kernels, local(): pl.pallas_call(functools.partial(front_kernel, *sizes), name='front', gri...  48.6 us
    pallas_call x1, Pallas kernels, local(): pl.pallas_call(functools.partial(back_kernel, *sizes), name='back', grid=...  15.1 us
    reshape x1, local copies, waits for them, and re-layouts, local(): row2 = lambda a: a.reshape(1, -1)  1.31 us

profile of v3, /device:TPU:1, one launch (start us, length us, event | category | flops | bytes accessed | tf_op | source)
XLA Modules:
  0.0 64.9 jit_solution(11088190073859145909)
XLA Ops:
  0.0 1.3 %reshape.17.cb_ref = f32[1,2304]{1,0:T(1,128)} reshape(f32[2304]{0:T(1024)} %param.12) | data formatting | bytes 18432 | tf_op jit(solution)/shard_map/reshape | solution.py:581
  1.3 48.6 %front.1 = (bf16[768,2048]{1,0:T(8,128)(2,1)}, bf16[768,2304]{1,0:T(8,128)(2,1)}, bf16[768,2304]{1,0:T(8,128)(2,1)}, bf16[768,2048]{1,0:T(8,128)(2,1)}, bf16[768...) custom-call(bf16[768,1024]{1,0:T(8,128)(2,1)} %x_ref.3, ...), custom_call_target="tpu_custom_call" | custom-call | tf_op jit(solution)/shard_map/front/pallas_call | solution.py:583
  49.9 15.1 %back.1 = bf16[768,1024]{1,0:T(8,128)(2,1)} custom-call(f32[2]{0:T(128)} %get-tuple-element.18.span_ref, bf16[768,2048]{1,0:T(8,128)(2,1)} %get-tuple-element.19.yf_ref, bf16[768,2048]{1,0:T(8,128)(2,1)} %get-tuple-element.20.yb_ref, bf16[768,2048]{1,0:T(8,128)(2,1)} %get-tuple-element.21.gate_ref, bf16[768,2304]{1,0:T(8,128)(2,1)} %get-tuple-element.22.cf_ref.xf_any, ...), custom_call_target="tpu_custom_call" | custom-call | tf_op jit(solution)/shard_map/back/pallas_call | solution.py:658

commit v4 on v3

--- a/solution.py
+++ b/solution.py
@@ -27,9 +27,12 @@
     return lax.dot_general(a, b, (((1,), (1,)), ((), ())), preferred_element_type=F32)
 
 
+def silu_of_half(half):
+    return half + half * jnp.tanh(half)
+
+
 def silu(x):
-    half = 0.5 * x
-    return half + half * jnp.tanh(half)
+    return silu_of_half(0.5 * x)
 
 
 def iota(shape, dim):
@@ -47,12 +50,6 @@
 def triangle(lower):
     row, column = time_of(iota((CHUNK, CHUNK), 0)), time_of(iota((CHUNK, CHUNK), 1))
     return row >= column if lower else row <= column
-
-
-def shuffle(inverse):
-    row, column = iota((CHUNK, CHUNK), 0), iota((CHUNK, CHUNK), 1)
-    hit = row == time_of(column) if inverse else time_of(row) == column
-    return jnp.where(hit, 1.0, 0.0).astype(BF16)
 
 
 def high_low(x):
@@ -66,15 +63,16 @@
     return [high, middle, x - high - middle]
 
 
-def spread_matrix(first, head_dim, depth):
-    row, column = iota_mod((depth, TILE), 0, 128), iota((depth, TILE), 1)
-    return jnp.where(row == first + lax.div(column, head_dim), 1.0, 0.0).astype(BF16)
+def spread_matrix(first, head_dim):
+    row, column = iota((128, TILE), 0), iota((128, TILE), 1)
+    half = jnp.where(row == first + lax.div(column, head_dim), 1.0, 0.0).astype(BF16)
+    return jnp.concatenate([half, half], 0)
 
 
 def front_kernel(
-    heads, head_dim, state, inner, x_ref, w_ref, wdt_ref, cw_ref, cb_ref, bias_ref, decay_ref, skip_ref,
-    gate_ref, xf_ref, xb_ref, yf_ref, yb_ref, sf_ref, sb_ref, in_ref, ef_ref, eb_ref, step_ref, off_ref, span_ref,
-    hx, xs, par, wf, wb, of, ob, gcf, gcb, btf, btb, small, rhs, kept_x, ends,
+    heads, head_dim, state, inner, x_ref, w_ref, wbc_ref, wdt_ref, cw_ref, cb_ref, bias_ref, decay_ref, skip_ref,
+    gate_ref, xf_ref, xb_ref, yf_ref, yb_ref, gf_ref, gb_ref, sf_ref, sb_ref, in_ref, step_ref, off_ref, span_ref,
+    hx, xs0, xs1, gate0, gate1, par, wf, wb, of, ob, update, gcf, gcb, btf, btb, small, rhs, kept_x, ends,
     follow, before_me, paired, chip, arrived, answers, entering, other, landed,
     halo_out, halo_in, pair_out, pair_in, first_out, first_in, second_out, second_in, back_out, back_in, own_sem,
 ):
@@ -170,35 +168,36 @@
             second_copy(k).start()
         pltpu.make_async_copy(answers.at[mine], entering.at[mine], own_sem.at[1]).start()
 
-    def back_copy():
-        return send(other, landed, back_out.at[0], back_in.at[0], partner)
+    def back_copy(k):
+        return send(other.at[k], landed.at[k], back_out.at[k], back_in.at[k], partner)
 
     def enter():
         pltpu.make_async_copy(answers.at[mine], entering.at[mine], own_sem.at[1]).wait()
-        for k in chips:
-            send(answers.at[k], entering.at[k], second_out.at[k], second_in.at[k], 2 * k + core).wait_recv()
-
-        def one_pair(k, _):
+
+        def one_pair(d, _):
+            k = lax.rem(mine + d, peers)
+
+            @pl.when(d > 0)
+            def _():
+                send(answers.at[k], entering.at[k], second_out.at[k], second_in.at[k], 2 * k + core).wait_recv()
+
             at = core * peers + k
             f_own, f_part = jnp.exp(total(ends, at)), jnp.exp(total(paired, k))
-            chip_f, chip_b = entering[k, 0].astype(F32), entering[k, 1].astype(F32)
-            own_late_f = f_part * chip_f + paired[k, 0, :state, :].astype(F32)
-            part_late_f = f_own * chip_f + ends[at, 0, :state, :].astype(F32)
-            own_late_b = f_part * chip_b + paired[k, 1, :state, :].astype(F32)
-            part_late_b = f_own * chip_b + ends[at, 1, :state, :].astype(F32)
-            in_ref[at, 0] = jnp.where(low, chip_f, own_late_f).astype(BF16)
-            other[k, 0] = jnp.where(low, part_late_f, chip_f).astype(BF16)
-            in_ref[at, 1] = jnp.where(low, own_late_b, chip_b).astype(BF16)
-            other[k, 1] = jnp.where(low, chip_b, part_late_b).astype(BF16)
+            one, none = jnp.ones_like(f_own), jnp.zeros_like(f_own)
+            for strand, early in ((0, low), (1, jnp.logical_not(low))):
+                chip_in = entering[k, strand].astype(F32)
+                scale, add = jnp.where(early, one, f_part), jnp.where(early, none, one)
+                in_ref[at, strand] = (scale * chip_in + add * paired[k, strand, :state, :].astype(F32)).astype(BF16)
+                scale, add = jnp.where(early, f_own, one), jnp.where(early, one, none)
+                other[k, strand] = (scale * chip_in + add * ends[at, strand, :state, :].astype(F32)).astype(BF16)
+            back_copy(k).start()
             return 0
 
         lax.fori_loop(0, peers, one_pair, 0)
-        back_copy().start()
 
     def finish():
-        back_copy().wait()
-
         def one_pair(k, _):
+            back_copy(k).wait()
             in_ref[(1 - core) * peers + k] = landed[k]
             return 0
 
@@ -211,10 +210,16 @@
             first_copy(k).wait_send()
             second_copy(k).wait_send()
 
-    def project():
-        out = dot_nt(hx[...], w_ref[...])
+    def keep_rows(xs, out):
         for c in range(chunks):
             xs[c * span + edge : c * span + edge + CHUNK] = out[c * CHUNK : (c + 1) * CHUNK]
+
+    def project(weights, xs):
+        out = dot_nt(hx[...], weights[...])
+        keep_rows(xs, out)
+        join(xs, out[length:])
+
+    def join(xs, out):
         sub = iota((8, TILE), 0)
 
         def rolled(c, r, by):
@@ -223,27 +228,27 @@
 
         for p in range(3):
             r = CHUNK // 8 - 3 + p
-            before = jnp.broadcast_to(out[length + 2 * HALO - 3 + p : length + 2 * HALO - 2 + p], (8, TILE))
+            before = jnp.broadcast_to(out[2 * HALO - 3 + p : 2 * HALO - 2 + p], (8, TILE))
             for c in range(chunks):
                 mine = rolled(c, r, 1)
                 xs[c * span + p * 8 : c * span + p * 8 + 8] = jnp.where(sub == 0, before, mine)
                 before = mine
-            after = jnp.broadcast_to(out[length + p : length + p + 1], (8, TILE))
+            after = jnp.broadcast_to(out[p : p + 1], (8, TILE))
             for c in reversed(range(chunks)):
                 mine = rolled(c, p, 7)
                 at = c * span + edge + CHUNK + p * 8
                 xs[at : at + 8] = jnp.where(sub == 7, after, mine)
                 after = mine
 
-    def convolved(c):
+    def convolved(xs, c):
         at = c * span + edge
-        taps = [cw_ref[k : k + 1, :] for k in range(4)]
-        base = xs[at : at + CHUNK] * taps[3] + cb_ref[...]
+        taps = [0.5 * cw_ref[k : k + 1, :] for k in range(4)]
+        base = xs[at : at + CHUNK] * taps[3] + 0.5 * cb_ref[...]
         forward, backward = base, base
         for k in range(1, 4):
             forward = forward + xs[at - 8 * k : at - 8 * k + CHUNK] * taps[3 - k]
             backward = backward + xs[at + 8 * k : at + 8 * k + CHUNK] * taps[3 - k]
-        return silu(forward), silu(backward)
+        return silu_of_half(forward), silu_of_half(backward)
 
     @pl.when(j == 0)
     def _():
@@ -254,7 +259,7 @@
         pl.semaphore_wait(barrier, peers + 1)
         for copy in halos():
             copy.start()
-        order = shuffle(False)
+        order = jnp.where(time_of(iota((CHUNK, CHUNK), 0)) == iota((CHUNK, CHUNK), 1), 1.0, 0.0).astype(BF16)
         for c in range(chunks):
             rows = slice(c * CHUNK, (c + 1) * CHUNK)
             hx[rows] = dot(order, x_ref[rows]).astype(BF16)
@@ -266,16 +271,16 @@
         lower = jnp.where(triangle(True), 1.0, 0.0)
         upper = jnp.where(triangle(False), 1.0, 0.0)
         lane1 = iota((1, 128), 1)
-        wdt = wdt_ref[...]
-        zero = jnp.zeros((128, wdt.shape[1]), BF16)
-        totals, kept = [], []
+        wdt = jnp.concatenate([wdt_ref[...], jnp.zeros((128 - heads, wdt_ref.shape[1]), BF16)], 0)
+        all_raw = dot_nt(hx[:length], wdt)
+        keep_rows(xs1, dot_nt(hx[:length], wbc_ref[...]))
+        totals = []
         for g in range(groups):
             members = range(g * packs, min((g + 1) * packs, chunks))
             raw = jnp.zeros((CHUNK, 128), F32)
             for q, c in enumerate(members):
-                parts = [zero[: q * heads], wdt, zero[: 128 - (q + 1) * heads]]
-                wide = jnp.concatenate([p for p in parts if p.shape[0]], 0)
-                raw = raw + dot_nt(hx[c * CHUNK : (c + 1) * CHUNK], wide)
+                one = all_raw[c * CHUNK : (c + 1) * CHUNK]
+                raw = raw + (pltpu.roll(one, q * heads, 1) if q else one)
             raw = raw.astype(BF16).astype(F32) + par[0:1, :]
             step = jnp.maximum(raw, 0.0) + jnp.log1p(jnp.exp(-jnp.abs(raw)))
             step = jnp.where(iota((CHUNK, 128), 1) < len(members) * heads, step, 0.0)
@@ -289,7 +294,6 @@
             of[g] = high_low(jnp.exp(jnp.minimum(head - total, 80.0)))
             ob[g] = high_low(jnp.exp(jnp.minimum(tail - total, 80.0)))
             totals.append(total)
-            kept.append((head, tail))
             span_ref[g] = -jnp.min(total)
 
         def wide8(x):
@@ -306,6 +310,7 @@
         slab = sums[0]
         for t in sums[1:]:
             slab = slab + t
+        reach = []
         for g in range(groups):
             t8 = wide8(totals[g])
             early, late = jnp.zeros((8, 128), F32), jnp.zeros((8, 128), F32)
@@ -321,13 +326,15 @@
             off_ref[g : g + 1, :] = early
             off_ref[groups + g : groups + g + 1, :] = late
             off_ref[2 * groups + 2 * g : 2 * groups + 2 * g + 2, :] = jnp.zeros((2, 128), F32)
-            ef_ref[g] = high_low(jnp.exp(kept[g][0] + early))
-            eb_ref[g] = high_low(jnp.exp(kept[g][1] + late))
+            reach.append((jnp.exp(early + totals[g]), jnp.exp(late + totals[g])))
         lines = []
         for g in range(groups):
             lines += three_terms(jnp.exp(totals[g]))
         lines += three_terms(slab) + three_terms(par[2:3, :])
-        lines.append(jnp.zeros((16 - len(lines), 128), F32))
+        for strand in range(2):
+            for g in range(groups):
+                lines += three_terms(reach[g][strand])
+        lines.append(jnp.zeros((small.shape[0] - len(lines), 128), F32))
         small[...] = jnp.concatenate(lines, 0).astype(BF16)
         for copy in halos():
             copy.wait_recv()
@@ -340,10 +347,10 @@
             ],
             0,
         ).astype(BF16)
-        project()
+        join(xs1, dot_nt(hx[length:], wbc_ref[...]))
         for c in range(chunks):
             rows = slice(c * CHUNK, (c + 1) * CHUNK)
-            forward, backward = convolved(c)
+            forward, backward = convolved(xs1, c)
             for value, out, gc, bt, keep in (
                 (forward, xf_ref, gcf, btf, triangle(True)),
                 (backward, xb_ref, gcb, btb, triangle(False)),
@@ -354,6 +361,7 @@
                 gc[rows, :CHUNK] = jnp.where(keep, dot_nt(c_part, b_part), 0.0).astype(BF16)
                 gc[rows, CHUNK:] = c_part
                 bt[rows, :] = value[:, :state].T.astype(BF16)
+        project(w_ref, xs0)
 
     first = lax.rem(j - 1, tiles) * (TILE // head_dim)
 
@@ -369,61 +377,103 @@
     def _():
         enter()
 
-    @pl.when((j > 0) & (j <= tiles))
-    def _():
+    def line_of(lines, q, k):
+        rows = lines[q][3 * k : 3 * k + 3]
+        return rows[0:1] + rows[1:2] + rows[2:3]
+
+    def gating(gate):
+        gate[...] = dot_nt(hx[:length], w_ref[...])
+
+    def values_step(xs):
         t = j - 1
-        project()
-        spreads = [spread_matrix(first + q * heads, head_dim, 256) for q in range(packs)]
+        spreads = [spread_matrix(first + q * heads, head_dim) for q in range(packs)]
         lines = [dot(small[...], spread[:128]) for spread in spreads]
-
-        def line(q, k):
-            rows = lines[q][3 * k : 3 * k + 3]
-            return rows[0:1] + rows[1:2] + rows[2:3]
-
-        fade = [line(c % packs, c // packs) for c in range(chunks)]
-        slab = line(0, groups)
+        fade = [line_of(lines, c % packs, c // packs) for c in range(chunks)]
+        slab = line_of(lines, 0, groups)
+
+        def summarise(c, pair):
+            for strand, (bt, scaled) in enumerate(zip((btf, btb), pair)):
+                update[strand, c] = dot(bt[c * CHUNK : (c + 1) * CHUNK, :], scaled)
+
+        scaled = None
         for c in range(chunks):
             rows = slice(c * CHUNK, (c + 1) * CHUNK)
-            g, spread = c // packs, spreads[c % packs]
-            for strand, (value, x_out, w) in enumerate(zip(convolved(c), (xf_ref, xb_ref), (wf, wb))):
+            weights = [dot(w[c // packs], spreads[c % packs]) for w in (wf, wb)]
+            if scaled is not None:
+                summarise(c - 1, scaled)
+            scaled = []
+            for strand, (value, x_out) in enumerate(zip(convolved(xs, c), (xf_ref, xb_ref))):
                 rounded = value.astype(BF16)
                 x_out[rows, :] = rounded
                 kept_x[strand, t, rows] = rounded
-                rhs[strand, t, c, :CHUNK] = (value * dot(w[g], spread)).astype(BF16)
+                scaled.append((value * weights[strand]).astype(BF16))
+                rhs[strand, t, c, :CHUNK] = scaled[strand]
+        summarise(chunks - 1, scaled)
         extra = jnp.concatenate(three_terms(slab) + [jnp.zeros((13, TILE), F32)], 0).astype(BF16)
-        for strand, (order, s_ref, bt) in enumerate(
-            ((range(chunks), sf_ref, btf), (reversed(range(chunks)), sb_ref, btb))
-        ):
+        for strand, (order, s_ref) in enumerate(((range(chunks), sf_ref), (reversed(range(chunks)), sb_ref))):
             running = jnp.zeros((state, TILE), F32)
             for c in order:
-                rows = slice(c * CHUNK, (c + 1) * CHUNK)
                 decayed = running * fade[c]
                 s_ref[c] = running.astype(BF16)
                 rhs[strand, t, c, CHUNK:] = decayed.astype(BF16)
-                running = decayed + dot(bt[rows, :], rhs[strand, t, c, :CHUNK])
+                running = decayed + update[strand, c]
             for half in range(per_tile):
                 lanes = slice(half * 128, (half + 1) * 128)
                 ends[t * per_tile + half, strand, :state, :] = running[:, lanes].astype(BF16)
                 ends[t * per_tile + half, strand, state:, :] = extra[:, lanes]
 
+    @pl.when((j > 0) & (j < tiles) & (lax.rem(j, 2) == 1))
+    def _():
+        project(w_ref, xs1)
+        values_step(xs0)
+
+    @pl.when((j > 0) & (j < tiles) & (lax.rem(j, 2) == 0))
+    def _():
+        project(w_ref, xs0)
+        values_step(xs1)
+
+    @pl.when(j == tiles)
+    def _():
+        gating(gate0)
+        values_step(xs1)
+
     @pl.when((j > 0) & (j <= tiles) & (lax.div(j - 1, half_tiles) != core))
     def _():
         pair_copy(j - 1).start()
 
-    @pl.when(j > tiles)
-    def _():
+    def outputs_step(gate):
         t = j - 1 - tiles
-        gate_ref[...] = dot_nt(hx[:length], w_ref[...]).astype(BF16)
-        spreads = [spread_matrix(first + q * heads, head_dim, 256) for q in range(packs)]
-        rows3 = dot(small[...], spreads[0][:128])[3 * groups + 3 : 3 * groups + 6]
-        skip = rows3[0:1] + rows3[1:2] + rows3[2:3]
+        spreads = [spread_matrix(first + q * heads, head_dim) for q in range(packs)]
+        lines = [dot(small[...], spread[:128]) for spread in spreads]
+        skip = line_of(lines, 0, groups + 1)
         for c in range(chunks):
             rows = slice(c * CHUNK, (c + 1) * CHUNK)
-            g, spread = c // packs, spreads[c % packs]
-            for strand, (y_ref, gc, o) in enumerate(((yf_ref, gcf, of), (yb_ref, gcb, ob))):
+            raw = gate[rows]
+            gate_ref[rows, :] = raw.astype(BF16)
+            open_gate = silu(raw)
+            for strand, (y_ref, g_ref, gc, o) in enumerate(
+                ((yf_ref, gf_ref, gcf, of), (yb_ref, gb_ref, gcb, ob))
+            ):
+                scale = dot(o[c // packs], spreads[c % packs]) * open_gate
                 mixed = dot(gc[rows, :], rhs[strand, t, c])
-                y = mixed * dot(o[g], spread) + skip * kept_x[strand, t, rows].astype(F32)
+                y = mixed * scale + (skip * open_gate) * kept_x[strand, t, rows].astype(F32)
                 y_ref[rows, :] = y.astype(BF16)
+                reach = line_of(lines, c % packs, (strand + 1) * groups + 2 + c // packs)
+                g_ref[rows, :] = (scale * reach).astype(BF16)
+
+    @pl.when((j > tiles) & (j < 2 * tiles) & (lax.rem(j, 2) == 1))
+    def _():
+        gating(gate1)
+        outputs_step(gate0)
+
+    @pl.when((j > tiles) & (j < 2 * tiles) & (lax.rem(j, 2) == 0))
+    def _():
+        gating(gate0)
+        outputs_step(gate1)
+
+    @pl.when(j == 2 * tiles)
+    def _():
+        outputs_step(gate1)
 
     @pl.when(j == 2 * tiles)
     def _():
@@ -435,9 +485,9 @@
 
 
 def back_kernel(
-    heads, head_dim, state, inner, span_ref, yf_ref, yb_ref, gate_ref, cf_ref, cb_ref, ef_ref, eb_ref, in_ref, x_ref,
-    w_ref, gain_ref, decay_ref, skip_ref, off_ref, xf_any, xb_any, sf_any, sb_any, step_any,
-    out_ref, gf, gb, accf, accb, normed, par, xbuf, sbuf, dtbuf, sem,
+    heads, head_dim, state, inner, span_ref, yf_ref, yb_ref, gf_ref, gb_ref, cf_ref, cb_ref, in_ref, x_ref,
+    w_ref, gain_ref, decay_ref, skip_ref, off_ref, gate_any, xf_any, xb_any, sf_any, sb_any, step_any,
+    out_ref, gf, gb, accf, accb, normed, unshuffled, par, xbuf, sbuf, dtbuf, gatebuf, sem,
 ):
     rows = out_ref.shape[0]
     i = pl.program_id(0)
@@ -454,22 +504,16 @@
         total_b = jnp.zeros((rows, 128), F32)
         for j in range(inner // TILE):
             lanes = slice(j * TILE, (j + 1) * TILE)
-            first = j * (TILE // head_dim)
-            spreads = [spread_matrix(first + (slot + k) * heads, head_dim, 256) for k in range(per_block)]
-            gate = silu(gate_ref[:, lanes].astype(F32))
-
-            def strand(y_ref, c_ref, e_ref, s, g):
+
+            def strand(y_ref, c_ref, g_ref, s, g):
                 entering = jnp.concatenate([in_ref[2 * j, s], in_ref[2 * j + 1, s]], 1)
-                y = y_ref[:, lanes].astype(F32) + jnp.concatenate([dot(e_ref[0], s) for s in spreads], 0) * dot(
-                    c_ref[...], entering
-                )
-                y = y * gate
+                y = y_ref[:, lanes].astype(F32) + g_ref[:, lanes].astype(F32) * dot(c_ref[...], entering)
                 g[:, lanes] = y
                 square = y * y
                 return square[:, :128] + square[:, 128:]
 
-            total_f = total_f + strand(yf_ref, cf_ref, ef_ref, 0, gf)
-            total_b = total_b + strand(yb_ref, cb_ref, eb_ref, 1, gb)
+            total_f = total_f + strand(yf_ref, cf_ref, gf_ref, 0, gf)
+            total_b = total_b + strand(yb_ref, cb_ref, gb_ref, 1, gb)
         accf[...] = total_f
         accb[...] = total_b
 
@@ -491,6 +535,7 @@
                     pltpu.make_async_copy(x_any.at[pl.ds(c * CHUNK, CHUNK)], xbuf, sem.at[0]),
                     pltpu.make_async_copy(s_any.at[c], sbuf, sem.at[1]),
                     pltpu.make_async_copy(step_any.at[group], dtbuf, sem.at[2]),
+                    pltpu.make_async_copy(gate_any.at[pl.ds(c * CHUNK, CHUNK)], gatebuf, sem.at[3]),
                 ]
                 for copy in copies:
                     copy.start()
@@ -527,7 +572,7 @@
                     carried = dot(c_part, entering.astype(BF16))
                     y = jnp.where(left, outs[0], outs[1]) + jnp.where(left, ups[0], ups[1]) * carried
                     y = y + jnp.where(lane1 < head_dim, skips[0], skips[1]) * v.astype(F32)
-                    y = y * silu(gate_ref[at, cols].astype(F32))
+                    y = y * silu(gatebuf[:, cols].astype(F32))
                     g[at, cols] = y
                     acc[at, :] += y * y
                     return 0
@@ -539,15 +584,19 @@
 
     scale_f = lax.rsqrt(jnp.sum(accf[...], 1, keepdims=True) * (1.0 / inner) + 1e-05)
     scale_b = lax.rsqrt(jnp.sum(accb[...], 1, keepdims=True) * (1.0 / inner) + 1e-05)
-    order = shuffle(True)
     for j in range(inner // TILE):
         lanes = slice(j * TILE, (j + 1) * TILE)
         value = (gf[:, lanes] * scale_f + gb[:, lanes] * scale_b) * gain_ref[:, lanes]
-        value = value.astype(BF16)
+        normed[:, lanes] = value.astype(BF16)
+    steps = CHUNK // 8
+    product = dot(normed[...], w_ref[...])
+    for n in range(w_ref.shape[1] // 128):
+        lanes = slice(n * 128, (n + 1) * 128)
         for k in range(per_block):
-            at = slice(k * CHUNK, (k + 1) * CHUNK)
-            normed[at, lanes] = dot(order, value[at]).astype(BF16)
-    out_ref[...] = (x_ref[...].astype(F32) + dot(normed[...], w_ref[...])).astype(BF16)
+            for r in range(steps):
+                at = k * CHUNK + r * 8
+                unshuffled[n, pl.ds(k * CHUNK + r, 8, stride=steps), :] = product[at : at + 8, lanes]
+        out_ref[:, lanes] = (x_ref[:, lanes].astype(F32) + unshuffled[n]).astype(BF16)
 
 
 def local(hidden, in_weight, conv_weight, conv_bias, step_bias, decay_rate, skip_gain, norm_gain, out_weight):
@@ -573,7 +622,10 @@
         return jnp.where(j == 0, tiles, value_tile(j))
 
     def weight_tile(j):
-        return jnp.where(j == 0, 2 * tiles, jnp.where(j <= tiles, tiles - 1 + j, j - tiles - 1))
+        return jnp.where(j < tiles, tiles + j, jnp.minimum(j - tiles, tiles - 1))
+
+    def out_tile(j):
+        return jnp.maximum(j - tiles - 1, 0)
 
     def shape(dims, dtype):
         return jax.ShapeDtypeStruct(dims, dtype)
@@ -587,6 +639,7 @@
         in_specs=[
             whole((length, width), **once),
             pl.BlockSpec((TILE, width), lambda j: (weight_tile(j), 0)),
+            pl.BlockSpec((TILE, width), lambda j: (2 * tiles, 0), **once),
             pl.BlockSpec((heads, width), lambda j: ((inner + conv_width) // heads, 0), **once),
             pl.BlockSpec((4, TILE), lambda j: (0, conv_tile(j))),
             pl.BlockSpec((1, TILE), lambda j: (0, conv_tile(j))),
@@ -595,16 +648,16 @@
             whole((1, heads)),
         ],
         out_specs=[
-            pl.BlockSpec((length, TILE), lambda j: (0, jnp.maximum(j - tiles - 1, 0))),
+            pl.BlockSpec((length, TILE), lambda j: (0, out_tile(j))),
             pl.BlockSpec((length, TILE), lambda j: (0, conv_tile(j))),
             pl.BlockSpec((length, TILE), lambda j: (0, conv_tile(j))),
-            pl.BlockSpec((length, TILE), lambda j: (0, jnp.maximum(j - tiles - 1, 0))),
-            pl.BlockSpec((length, TILE), lambda j: (0, jnp.maximum(j - tiles - 1, 0))),
+            pl.BlockSpec((length, TILE), lambda j: (0, out_tile(j))),
+            pl.BlockSpec((length, TILE), lambda j: (0, out_tile(j))),
+            pl.BlockSpec((length, TILE), lambda j: (0, out_tile(j))),
+            pl.BlockSpec((length, TILE), lambda j: (0, out_tile(j))),
             pl.BlockSpec((chunks, state, TILE), lambda j: (0, 0, value_tile(j))),
             pl.BlockSpec((chunks, state, TILE), lambda j: (0, 0, value_tile(j))),
             whole((count, 2, state, 128)),
-            whole((groups, CHUNK, 256)),
-            whole((groups, CHUNK, 256)),
             whole((groups, CHUNK, 128)),
             whole((4 * groups, 128)),
             pl.BlockSpec(memory_space=pltpu.SMEM),
@@ -615,11 +668,11 @@
             shape((length, conv_width), BF16),
             shape((length, inner), BF16),
             shape((length, inner), BF16),
+            shape((length, inner), BF16),
+            shape((length, inner), BF16),
             shape((chunks, state, inner), BF16),
             shape((chunks, state, inner), BF16),
             shape((count, 2, state, 128), BF16),
-            shape((groups, CHUNK, 256), BF16),
-            shape((groups, CHUNK, 256), BF16),
             shape((groups, CHUNK, 128), F32),
             shape((4 * groups, 128), F32),
             shape((groups,), F32),
@@ -627,12 +680,16 @@
         scratch_shapes=[
             pltpu.VMEM((length + 2 * HALO, width), BF16),
             pltpu.VMEM((chunks * (CHUNK + 48), TILE), F32),
+            pltpu.VMEM((chunks * (CHUNK + 48), TILE), F32),
+            pltpu.VMEM((length, TILE), F32),
+            pltpu.VMEM((length, TILE), F32),
             pltpu.VMEM((8, 128), F32),
         ]
         + [pltpu.VMEM((groups, CHUNK, 256), BF16)] * 4
+        + [pltpu.VMEM((2, chunks, state, TILE), F32)]
         + [pltpu.VMEM((length, CHUNK + state), BF16)] * 2
         + [pltpu.VMEM((chunks * state, CHUNK), BF16)] * 2
-        + [pltpu.VMEM((16, 128), BF16)]
+        + [pltpu.VMEM((32, 128), BF16)]
         + [
             pltpu.VMEM((2, tiles, chunks, CHUNK + state, TILE), BF16),
             pltpu.VMEM((2, tiles, length, TILE), BF16),
@@ -644,24 +701,23 @@
         + [pltpu.VMEM((count // 2, 2, state, 128), BF16)] * 4
         + [pltpu.SemaphoreType.DMA((n,)) for n in (2, 2, tiles // 2, tiles // 2)]
         + [pltpu.SemaphoreType.DMA((count // 2,))] * 4
-        + [pltpu.SemaphoreType.DMA((n,)) for n in (1, 1, 2)],
+        + [pltpu.SemaphoreType.DMA((n,)) for n in (count // 2, count // 2, 2)],
         compiler_params=pltpu.CompilerParams(collective_id=0, has_side_effects=True, vmem_limit_bytes=VMEM),
     )(
-        hidden, in_weight.T, in_weight.T, conv_weight, row2(conv_bias), row2(step_bias), row2(decay_rate),
+        hidden, in_weight.T, in_weight.T, in_weight.T, conv_weight, row2(conv_bias), row2(step_bias), row2(decay_rate),
         row2(skip_gain),
     )
-    gate, xf, xb, yf, yb, sf, sb, entering, ef, eb, step, off, span = outs
+    gate, xf, xb, yf, yb, gf, gb, sf, sb, entering, step, off, span = outs
     anywhere = pl.BlockSpec(memory_space=pl.ANY)
     block = pl.BlockSpec((ROWS, inner), lambda j: (j, 0))
     c_block = pl.BlockSpec((ROWS, state), lambda j: (j, inner // state + 1))
-    e_block = pl.BlockSpec((1, CHUNK, 256), lambda j: (j * (ROWS // CHUNK) // (128 // heads), 0, 0))
     return pl.pallas_call(
         functools.partial(back_kernel, *sizes),
         name="back",
         grid=(length // ROWS,),
         in_specs=[
             pl.BlockSpec(memory_space=pltpu.SMEM),
-            block, block, block, c_block, c_block, e_block, e_block,
+            block, block, block, block, c_block, c_block,
             whole((count, 2, state, 128), **once),
             pl.BlockSpec((ROWS, width), lambda j: (j, 0)),
             whole((inner, width), **once),
@@ -670,7 +726,7 @@
             whole((1, heads)),
             whole((4 * groups, 128)),
         ]
-        + [anywhere] * 5,
+        + [anywhere] * 6,
         out_specs=pl.BlockSpec((ROWS, width), lambda j: (j, 0)),
         out_shape=shape((length, width), BF16),
         scratch_shapes=[
@@ -679,16 +735,18 @@
             pltpu.VMEM((ROWS, 128), F32),
             pltpu.VMEM((ROWS, 128), F32),
             pltpu.VMEM((ROWS, inner), BF16),
+            pltpu.VMEM((width // 128, ROWS, 128), F32),
             pltpu.VMEM((8, 128), F32),
             pltpu.VMEM((CHUNK, conv_width), BF16),
             pltpu.VMEM((state, inner), BF16),
             pltpu.VMEM((CHUNK, 128), F32),
-            pltpu.SemaphoreType.DMA((3,)),
+            pltpu.VMEM((CHUNK, inner), BF16),
+            pltpu.SemaphoreType.DMA((4,)),
         ],
         compiler_params=pltpu.CompilerParams(vmem_limit_bytes=VMEM),
     )(
-        span, yf, yb, gate, xf, xb, ef, eb, entering, hidden, out_weight, row2(norm_gain), row2(decay_rate),
-        row2(skip_gain), off, xf, xb, sf, sb, step,
+        span, yf, yb, gf, gb, xf, xb, entering, hidden, out_weight, row2(norm_gain), row2(decay_rate),
+        row2(skip_gain), off, gate, xf, xb, sf, sb, step,
     )
 
 

time: 65.3 us -> 59.6 us (0.913)
  Pallas kernels: 63.6 us -> 57.8 us
    pallas_call x1, Pallas kernels: 48.6 us -> 43.9 us  [local(): pl.pallas_call(functools.partial(front_kernel, *sizes), name='front', gri...]
    pallas_call x1, Pallas kernels: 15.1 us -> 13.9 us  [local(): pl.pallas_call(functools.partial(back_kernel, *sizes), name='back', grid=...]
where the time goes in v4:
time: 59.6 us; the launch traced here: 59.3 us
  Pallas kernels  57.8 us (97%)
  local copies, waits for them, and re-layouts  1.31 us (2%)
    pallas_call x1, Pallas kernels, local(): pl.pallas_call(functools.partial(front_kernel, *sizes), name='front', gri...  43.9 us
    pallas_call x1, Pallas kernels, local(): pl.pallas_call(functools.partial(back_kernel, *sizes), name='back', grid=...  13.9 us
    reshape x1, local copies, waits for them, and re-layouts, local(): row2 = lambda a: a.reshape(1, -1)  1.31 us

profile of v4, /device:TPU:1, one launch (start us, length us, event | category | flops | bytes accessed | tf_op | source)
XLA Modules:
  0.0 59.3 jit_solution(16174860514428340090)
XLA Ops:
  0.0 1.3 %reshape.17.cb_ref = f32[1,2304]{1,0:T(1,128)} reshape(f32[2304]{0:T(1024)} %param.12) | data formatting | bytes 18432 | tf_op jit(solution)/shard_map/reshape | solution.py:633
  1.3 43.9 %front.1 = (bf16[768,2048]{1,0:T(8,128)(2,1)}, bf16[768,2304]{1,0:T(8,128)(2,1)}, bf16[768,2304]{1,0:T(8,128)(2,1)}, bf16[768,2048]{1,0:T(8,128)(2,1)}, bf16[768...) custom-call(bf16[768,1024]{1,0:T(8,128)(2,1)} %x_ref.3, ...), custom_call_target="tpu_custom_call" | custom-call | tf_op jit(solution)/shard_map/front/pallas_call | solution.py:635
  45.2 13.9 %back.1 = bf16[768,1024]{1,0:T(8,128)(2,1)} custom-call(f32[2]{0:T(128)} %get-tuple-element.18.span_ref, bf16[768,2048]{1,0:T(8,128)(2,1)} %get-tuple-element.19.yf_ref, bf16[768,2048]{1,0:T(8,128)(2,1)} %get-tuple-element.20.yb_ref, bf16[768,2048]{1,0:T(8,128)(2,1)} %get-tuple-element.21.gf_ref, bf16[768,2048]{1,0:T(8,128)(2,1)} %get-tuple-element.22.gb_ref, ...), custom_call_target="tpu_custom_call" | custom-call | tf_op jit(solution)/shard_map/back/pallas_call | solution.py:714

commit v5 on v4

--- a/solution.py
+++ b/solution.py
@@ -240,10 +240,13 @@
                 xs[at : at + 8] = jnp.where(sub == 7, after, mine)
                 after = mine
 
+    conv_at = jnp.where(j == 0, tiles, jnp.clip(j - 1, 0, tiles - 1)) * per_tile
+    bias = jnp.concatenate([cb_ref[pl.ds(conv_at + n, 1), :] for n in range(per_tile)], 1)
+
     def convolved(xs, c):
         at = c * span + edge
         taps = [0.5 * cw_ref[k : k + 1, :] for k in range(4)]
-        base = xs[at : at + CHUNK] * taps[3] + 0.5 * cb_ref[...]
+        base = xs[at : at + CHUNK] * taps[3] + 0.5 * bias
         forward, backward = base, base
         for k in range(1, 4):
             forward = forward + xs[at - 8 * k : at - 8 * k + CHUNK] * taps[3 - k]
@@ -369,11 +372,11 @@
     def _():
         combine(j - 2)
 
-    @pl.when(j == tiles + 1 + core * half_tiles)
+    @pl.when(j == tiles + core * half_tiles)
     def _():
         scan()
 
-    @pl.when((j == tiles + 1 + half_tiles) & low)
+    @pl.when((j == tiles + half_tiles) & low)
     def _():
         enter()
 
@@ -586,7 +589,8 @@
     scale_b = lax.rsqrt(jnp.sum(accb[...], 1, keepdims=True) * (1.0 / inner) + 1e-05)
     for j in range(inner // TILE):
         lanes = slice(j * TILE, (j + 1) * TILE)
-        value = (gf[:, lanes] * scale_f + gb[:, lanes] * scale_b) * gain_ref[:, lanes]
+        gain = jnp.concatenate([gain_ref[n : n + 1, :] for n in range(2 * j, 2 * j + 2)], 1)
+        value = (gf[:, lanes] * scale_f + gb[:, lanes] * scale_b) * gain
         normed[:, lanes] = value.astype(BF16)
     steps = CHUNK // 8
     product = dot(normed[...], w_ref[...])
@@ -642,7 +646,7 @@
             pl.BlockSpec((TILE, width), lambda j: (2 * tiles, 0), **once),
             pl.BlockSpec((heads, width), lambda j: ((inner + conv_width) // heads, 0), **once),
             pl.BlockSpec((4, TILE), lambda j: (0, conv_tile(j))),
-            pl.BlockSpec((1, TILE), lambda j: (0, conv_tile(j))),
+            whole((conv_width // 128, 128)),
             whole((1, heads)),
             whole((1, heads)),
             whole((1, heads)),
@@ -704,7 +708,7 @@
         + [pltpu.SemaphoreType.DMA((n,)) for n in (count // 2, count // 2, 2)],
         compiler_params=pltpu.CompilerParams(collective_id=0, has_side_effects=True, vmem_limit_bytes=VMEM),
     )(
-        hidden, in_weight.T, in_weight.T, in_weight.T, conv_weight, row2(conv_bias), row2(step_bias), row2(decay_rate),
+        hidden, in_weight.T, in_weight.T, in_weight.T, conv_weight, conv_bias.reshape(-1, 128), row2(step_bias), row2(decay_rate),
         row2(skip_gain),
     )
     gate, xf, xb, yf, yb, gf, gb, sf, sb, entering, step, off, span = outs
@@ -721,7 +725,7 @@
             whole((count, 2, state, 128), **once),
             pl.BlockSpec((ROWS, width), lambda j: (j, 0)),
             whole((inner, width), **once),
-            whole((1, inner)),
+            whole((inner // 128, 128)),
             whole((1, heads)),
             whole((1, heads)),
             whole((4 * groups, 128)),
@@ -745,7 +749,7 @@
         ],
         compiler_params=pltpu.CompilerParams(vmem_limit_bytes=VMEM),
     )(
-        span, yf, yb, gf, gb, xf, xb, entering, hidden, out_weight, row2(norm_gain), row2(decay_rate),
+        span, yf, yb, gf, gb, xf, xb, entering, hidden, out_weight, norm_gain.reshape(-1, 128), row2(decay_rate),
         row2(skip_gain), off, gate, xf, xb, sf, sb, step,
     )
 

time: 59.6 us -> 58.6 us (0.983)
  local copies, waits for them, and re-layouts: 1.31 us -> 0 us
    reshape x1 -> x0, local copies, waits for them, and re-layouts: 1.31 us -> none  [local(): row2 = lambda a: a.reshape(1, -1)]
where the time goes in v5:
time: 58.6 us; the launch traced here: 58.1 us
  Pallas kernels  57.9 us (99%)
    pallas_call x1, Pallas kernels, local(): pl.pallas_call(functools.partial(front_kernel, *sizes), name='front', gri...  44 us
    pallas_call x1, Pallas kernels, local(): pl.pallas_call(functools.partial(back_kernel, *sizes), name='back', grid=...  13.9 us

profile of v5, /device:TPU:1, one launch (start us, length us, event | category | flops | bytes accessed | tf_op | source)
XLA Modules:
  0.0 58.1 jit_solution(766157800298855063)
XLA Ops:
  0.0 44.0 %front.1 = (bf16[768,2048]{1,0:T(8,128)(2,1)}, bf16[768,2304]{1,0:T(8,128)(2,1)}, bf16[768,2304]{1,0:T(8,128)(2,1)}, bf16[768,2048]{1,0:T(8,128)(2,1)}, bf16[768...) custom-call(bf16[768,1024]{1,0:T(8,128)(2,1)} %x_ref.3, ...), custom_call_target="tpu_custom_call" | custom-call | tf_op jit(solution)/shard_map/front/pallas_call | solution.py:639
  44.0 13.9 %back.1 = bf16[768,1024]{1,0:T(8,128)(2,1)} custom-call(f32[2]{0:T(128)} %get-tuple-element.18.span_ref, bf16[768,2048]{1,0:T(8,128)(2,1)} %get-tuple-element.19.yf_ref, bf16[768,2048]{1,0:T(8,128)(2,1)} %get-tuple-element.20.yb_ref, bf16[768,2048]{1,0:T(8,128)(2,1)} %get-tuple-element.21.gf_ref, bf16[768,2048]{1,0:T(8,128)(2,1)} %get-tuple-element.22.gb_ref, ...), custom_call_target="tpu_custom_call" | custom-call | tf_op jit(solution)/shard_map/back/pallas_call | solution.py:718
